TPU v7x, 256 devices: a whole 4x4x8 slice. The times are simulated.
256 devices in a mesh: row: 16 (over y, z_hi), col: 16 (over x, z_lo, core).
Axes of the slice: x: 4, y: 4, z: 8 (z_hi: 4, z_lo: 2; z = z_hi * 2 + z_lo), core: 2. Of those that a mesh axis runs over, the one named last changes fastest.
Arguments:
- features: bfloat16 [65536, 256], P(('col', 'row')), may hold values from -6 to 6
- weight: bfloat16 [256, 256], replicated, may hold values from -0.375 to 0.375
- tile_rows: int32 [16, 16, 320], P('row', 'col'), may hold values from 0 to 31, as said below
- tile_cols: int32 [16, 16, 320], P('row', 'col'), may hold values from 0 to 31
- tile_count: int32 [16, 16], P('row', 'col'), may hold values from 40 to 320, as said below
- tile_values: bfloat16 [16, 16, 320, 128, 128], P('row', 'col'), may hold values from 0.0019989014 to 0.049804688
- grad_out: bfloat16 [65536, 256], P(('row', 'col')), may hold values from -6 to 6
Outputs:
- activations: bfloat16 [65536, 256], P(('row', 'col'))
- feature_grad: bfloat16 [65536, 256], P(('col', 'row'))
- weight_grad: float32 [256, 256], replicated
Inputs may be any that keep to these rules, and one draw needn't show every extreme that they name: `tile_rows`: the first tile_count slots of a device name distinct tiles. `tile_count`: slots at or after a device's count are unused and their rows, columns and values are ignored; some device uses all 320 slots in every draw.
All inputs are finite; a program needn't handle non-finite values.
Results may differ from a plain program's by a relative error of at most 0.027.
Values may be sent and summed in bfloat16 or wider, within the bound.
No kernel may reach another device: no remote copies, remote signals or barrier semaphores. Data moves between devices by JAX's collectives and lax.ppermute only.
A program may use at most 128 MiB of HBM per device.

v0:
```python
import math

import jax
import jax.numpy as jnp
from jax import lax
from jax.sharding import PartitionSpec as P


def gelu_tanh(value):
    return jax.nn.gelu(value, approximate=True)


def tile_products(block_tiles, put_ids, take_ids, live_count, source, out_blocks, transpose):
    slot_total = block_tiles.shape[0]
    tile_size = block_tiles.shape[1]
    feat_width = source.shape[1]
    block_slots = math.gcd(slot_total, 64)
    source_tiles = source.reshape(-1, tile_size, feat_width)

    def one_block(running_sum, first_slot):
        block_values = lax.dynamic_slice_in_dim(block_tiles, first_slot, block_slots, 0)
        take_index = lax.dynamic_slice_in_dim(take_ids, first_slot, block_slots, 0)
        put_index = lax.dynamic_slice_in_dim(put_ids, first_slot, block_slots, 0)
        picked = source_tiles[take_index]
        if transpose:
            products = jnp.einsum(
                "kab,kaf->kbf", block_values, picked, preferred_element_type=jnp.float32
            )
        else:
            products = jnp.einsum(
                "kab,kbf->kaf", block_values, picked, preferred_element_type=jnp.float32
            )
        slot_numbers = first_slot + jnp.arange(block_slots, dtype=jnp.int32)
        live_slots = (slot_numbers < live_count).astype(jnp.float32)
        running_sum = running_sum.at[put_index].add(products * live_slots[:, None, None])
        return (running_sum, None)

    starts = jnp.arange(0, slot_total, block_slots, dtype=jnp.int32)
    empty = jnp.zeros((out_blocks, tile_size, feat_width), jnp.float32)
    running_sum, _ = lax.scan(one_block, empty, starts)
    return running_sum.reshape(out_blocks * tile_size, feat_width)


def on_device(features, weight, tile_rows, tile_cols, tile_count, tile_values, grad_out):
    seg_rows, feat_width = features.shape
    tile_size = tile_values.shape[-1]
    block_tiles = tile_values[0, 0]
    tile_row_ids = tile_rows[0, 0]
    tile_col_ids = tile_cols[0, 0]
    live_count = tile_count[0, 0]
    row_blocks = lax.axis_size("col") * seg_rows // tile_size
    col_blocks = lax.axis_size("row") * seg_rows // tile_size
    node_total = seg_rows * lax.axis_size("row") * lax.axis_size("col")
    projected = jnp.dot(features, weight, preferred_element_type=jnp.float32).astype(jnp.bfloat16)
    gathered = lax.all_gather(projected, "row", axis=0, tiled=True)
    partial_value = tile_products(
        block_tiles, tile_row_ids, tile_col_ids, live_count, gathered, row_blocks, False
    )
    summed = lax.psum_scatter(
        partial_value.astype(jnp.bfloat16), "col", scatter_dimension=0, tiled=True
    ).astype(jnp.float32)
    activations, pullback = jax.vjp(gelu_tanh, summed)
    gradient = pullback(grad_out.astype(jnp.float32))[0].astype(jnp.bfloat16)
    activations = activations.astype(jnp.bfloat16)
    grad_blocks = lax.all_gather(gradient, "col", axis=0, tiled=True)
    partial_back = tile_products(
        block_tiles, tile_col_ids, tile_row_ids, live_count, grad_blocks, col_blocks, True
    )
    back_sum = lax.psum_scatter(
        partial_back.astype(jnp.bfloat16), "row", scatter_dimension=0, tiled=True
    ).astype(jnp.float32)
    back_sum = back_sum.astype(jnp.bfloat16)
    feature_grad = lax.dot_general(
        back_sum, weight, (((1,), (1,)), ((), ())), preferred_element_type=jnp.float32
    ).astype(jnp.bfloat16)
    local_weight = lax.dot_general(
        features, back_sum, (((0,), (0,)), ((), ())), preferred_element_type=jnp.float32
    )
    weight_grad = lax.psum(local_weight, ("row", "col")) * (1.0 / math.sqrt(node_total))
    return (activations, feature_grad, weight_grad)


def solution(mesh):
    placed = (
        P(("col", "row"), None),
        P(),
        P("row", "col", None),
        P("row", "col", None),
        P("row", "col"),
        P("row", "col", None, None, None),
        P(("row", "col"), None),
    )
    return jax.shard_map(
        on_device,
        mesh=mesh,
        in_specs=placed,
        out_specs=(P(("row", "col"), None), P(("col", "row"), None), P()),
        check_vma=False,
    )
```

profile of v0, /device:TPU:2, one launch (start us, length us, event | category | flops | bytes accessed | tf_op | source)
XLA Modules:
  0.0 872.9 jit_solution(571299190547295422)
XLA Ops:
  7.2 0.8 copy-done
  8.1 1.7 convolution_convert_fusion.1
  9.9 0.7 reduce
  10.6 0.7 reduce.1
  11.3 61.9 %all-gather.3.cloned.1.call-done = bf16[4096,256]{1,0:T(8,128)(2,1)} async-done(((bf16[256,256]{1,0:T(8,128)(2,1)}), bf16[4096,256]{1,0:T(8,128)(2,1)}) %all-gather.3.cloned.1.call-update) | async-done | bytes 2097168 | tf_op jit(solution)/shard_map/all_gather | solution.py:55
  73.2 2.4 broadcast.47.clone
  75.6 165.6 %while.20 = (s32[]{:T(128)}, f32[32,128,256]{2,1,0:T(8,128)}, s32[5]{0:T(128)S(1)}, s32[320]{0:T(512)S(1)}, bf16[320,128,128]{2,1,0:T(8,128)(2,1)}, /*index=5*/s...) while((s32[]{:T(128)}, f32[32,128,256]{2,1,0:T(8,128)}, ...), condition=%wide.region_2.3_spmd, body=%wide.region_0.2_spmd.sunk | while | flops 541066816 | bytes 48241072 | solution.py:40
  75.6 0.6 dynamic_slice.41
  78.1 1.3 compare_convert_fusion.4
  79.5 2.7 gather_fusion
  82.3 7.3 broadcast_multiply_fusion.5
  89.6 19.1 %scatter_fusion = f32[32,128,256]{2,1,0:T(8,128)} fusion(f32[32,128,256]{2,1,0:T(8,128)} %get-tuple-element.256, s32[64]{0:T(128)S(1)} %get-tuple-element.232, f32[64,128,256]{2,1,0:T(8,128)} %broadcast_multiply_fusion.5), kind=kCustom, calls=%fused_computation.2.clone.1 | custom fusion | flops 2097152 | bytes 25166080 | tf_op jit(solution)/shard_map/while/body/eval_jaxpr/scatter-add | solution.py:35
  111.2 1.3 compare_convert_fusion.4
  112.6 2.7 gather_fusion
  115.3 7.3 broadcast_multiply_fusion.5
  122.6 19.1 %scatter_fusion = f32[32,128,256]{2,1,0:T(8,128)} fusion(f32[32,128,256]{2,1,0:T(8,128)} %get-tuple-element.256, s32[64]{0:T(128)S(1)} %get-tuple-element.232, f32[64,128,256]{2,1,0:T(8,128)} %broadcast_multiply_fusion.5), kind=kCustom, calls=%fused_computation.2.clone.1 | custom fusion | flops 2097152 | bytes 25166080 | tf_op jit(solution)/shard_map/while/body/eval_jaxpr/scatter-add | solution.py:35
  144.3 1.3 compare_convert_fusion.4
  145.7 2.7 gather_fusion
  148.4 7.3 broadcast_multiply_fusion.5
  155.7 19.0 %scatter_fusion = f32[32,128,256]{2,1,0:T(8,128)} fusion(f32[32,128,256]{2,1,0:T(8,128)} %get-tuple-element.256, s32[64]{0:T(128)S(1)} %get-tuple-element.232, f32[64,128,256]{2,1,0:T(8,128)} %broadcast_multiply_fusion.5), kind=kCustom, calls=%fused_computation.2.clone.1 | custom fusion | flops 2097152 | bytes 25166080 | tf_op jit(solution)/shard_map/while/body/eval_jaxpr/scatter-add | solution.py:35
  177.2 1.3 compare_convert_fusion.4
  178.6 2.7 gather_fusion
  181.4 7.3 broadcast_multiply_fusion.5
  188.7 19.3 %scatter_fusion = f32[32,128,256]{2,1,0:T(8,128)} fusion(f32[32,128,256]{2,1,0:T(8,128)} %get-tuple-element.256, s32[64]{0:T(128)S(1)} %get-tuple-element.232, f32[64,128,256]{2,1,0:T(8,128)} %broadcast_multiply_fusion.5), kind=kCustom, calls=%fused_computation.2.clone.1 | custom fusion | flops 2097152 | bytes 25166080 | tf_op jit(solution)/shard_map/while/body/eval_jaxpr/scatter-add | solution.py:35
  210.4 1.3 compare_convert_fusion.4
  211.8 2.7 gather_fusion
  214.6 7.3 broadcast_multiply_fusion.5
  221.9 19.3 %scatter_fusion = f32[32,128,256]{2,1,0:T(8,128)} fusion(f32[32,128,256]{2,1,0:T(8,128)} %get-tuple-element.256, s32[64]{0:T(128)S(1)} %get-tuple-element.232, f32[64,128,256]{2,1,0:T(8,128)} %broadcast_multiply_fusion.5), kind=kCustom, calls=%fused_computation.2.clone.1 | custom fusion | flops 2097152 | bytes 25166080 | tf_op jit(solution)/shard_map/while/body/eval_jaxpr/scatter-add | solution.py:35
  241.2 3.8 convert_element_type.47
  245.1 58.5 %reduce-scatter.3.cloned.1.call-done = bf16[256,256]{1,0:T(8,128)(2,1)} async-done(((bf16[4096,256]{1,0:T(8,128)(2,1)}), bf16[256,256]{1,0:T(8,128)(2,1)}) %reduce-scatter.3.cloned.1.call-update) | async-done | bytes 131088 | tf_op jit(solution)/shard_map/reduce_scatter | solution.py:59
  303.6 1.8 fusion.7
  305.5 14.4 %copy.10 = bf16[1,1,320,128,128]{3,4,2,1,0:T(8,128)(2,1)} copy(bf16[1,1,320,128,128]{4,3,2,1,0:T(8,128)(2,1)} %bitcast.30) | data formatting | bytes 20971520 | tf_op args[5]
  319.9 27.7 %all-gather.5.cloned.1.call-done = bf16[4096,256]{1,0:T(8,128)(2,1)} async-done(((bf16[256,256]{1,0:T(8,128)(2,1)}), bf16[4096,256]{1,0:T(8,128)(2,1)}) %all-gather.5.cloned.1.call-update) | async-done | bytes 2097168 | tf_op jit(solution)/shard_map/all_gather | solution.py:65
  347.6 2.5 broadcast.47
  350.1 167.4 %while.21 = (s32[]{:T(128)}, f32[32,128,256]{2,1,0:T(8,128)}, s32[5]{0:T(128)S(1)}, s32[320]{0:T(512)S(1)}, bf16[320,128,128]{1,2,0:T(8,128)(2,1)}, /*index=5*/s...) while((s32[]{:T(128)}, f32[32,128,256]{2,1,0:T(8,128)}, ...), condition=%wide.region_6.7_spmd, body=%wide.region_4.6_spmd.sunk | while | flops 541066816 | bytes 48241072 | solution.py:40
  350.1 0.6 dynamic_slice.44
  352.6 1.3 compare_convert_fusion.5
  354.0 2.8 gather_fusion.1
  356.9 7.4 broadcast_multiply_fusion.6
  364.2 19.3 %scatter_fusion.1 = f32[32,128,256]{2,1,0:T(8,128)} fusion(f32[32,128,256]{2,1,0:T(8,128)} %get-tuple-element.289, s32[64]{0:T(128)S(1)} %get-tuple-element.242, f32[64,128,256]{2,1,0:T(8,128)} %broadcast_multiply_fusion.6), kind=kCustom, calls=%fused_computation.3.clone.1 | custom fusion | flops 2097152 | bytes 25166080 | tf_op jit(solution)/shard_map/while/body/eval_jaxpr/scatter-add | solution.py:35
  386.0 1.3 compare_convert_fusion.5
  387.4 2.8 gather_fusion.1
  390.3 7.4 broadcast_multiply_fusion.6
  397.6 19.5 %scatter_fusion.1 = f32[32,128,256]{2,1,0:T(8,128)} fusion(f32[32,128,256]{2,1,0:T(8,128)} %get-tuple-element.289, s32[64]{0:T(128)S(1)} %get-tuple-element.242, f32[64,128,256]{2,1,0:T(8,128)} %broadcast_multiply_fusion.6), kind=kCustom, calls=%fused_computation.3.clone.1 | custom fusion | flops 2097152 | bytes 25166080 | tf_op jit(solution)/shard_map/while/body/eval_jaxpr/scatter-add | solution.py:35
  417.1 0.6 dynamic_slice.44
  419.7 1.3 compare_convert_fusion.5
  421.1 2.8 gather_fusion.1
  423.9 7.4 broadcast_multiply_fusion.6
  431.3 19.4 %scatter_fusion.1 = f32[32,128,256]{2,1,0:T(8,128)} fusion(f32[32,128,256]{2,1,0:T(8,128)} %get-tuple-element.289, s32[64]{0:T(128)S(1)} %get-tuple-element.242, f32[64,128,256]{2,1,0:T(8,128)} %broadcast_multiply_fusion.6), kind=kCustom, calls=%fused_computation.3.clone.1 | custom fusion | flops 2097152 | bytes 25166080 | tf_op jit(solution)/shard_map/while/body/eval_jaxpr/scatter-add | solution.py:35
  453.2 1.3 compare_convert_fusion.5
  454.6 2.8 gather_fusion.1
  457.4 7.4 broadcast_multiply_fusion.6
  464.8 19.3 %scatter_fusion.1 = f32[32,128,256]{2,1,0:T(8,128)} fusion(f32[32,128,256]{2,1,0:T(8,128)} %get-tuple-element.289, s32[64]{0:T(128)S(1)} %get-tuple-element.242, f32[64,128,256]{2,1,0:T(8,128)} %broadcast_multiply_fusion.6), kind=kCustom, calls=%fused_computation.3.clone.1 | custom fusion | flops 2097152 | bytes 25166080 | tf_op jit(solution)/shard_map/while/body/eval_jaxpr/scatter-add | solution.py:35
  486.6 1.3 compare_convert_fusion.5
  487.9 2.8 gather_fusion.1
  490.8 7.4 broadcast_multiply_fusion.6
  498.1 19.3 %scatter_fusion.1 = f32[32,128,256]{2,1,0:T(8,128)} fusion(f32[32,128,256]{2,1,0:T(8,128)} %get-tuple-element.289, s32[64]{0:T(128)S(1)} %get-tuple-element.242, f32[64,128,256]{2,1,0:T(8,128)} %broadcast_multiply_fusion.6), kind=kCustom, calls=%fused_computation.3.clone.1 | custom fusion | flops 2097152 | bytes 25166080 | tf_op jit(solution)/shard_map/while/body/eval_jaxpr/scatter-add | solution.py:35
  517.5 3.8 convert_element_type.53
  521.4 88.9 %reduce-scatter.5.cloned.1.call-done = bf16[256,256]{1,0:T(8,128)(2,1)} async-done(((bf16[4096,256]{1,0:T(8,128)(2,1)}), bf16[256,256]{1,0:T(8,128)(2,1)}) %reduce-scatter.5.cloned.1.call-update) | async-done | bytes 131088 | tf_op jit(solution)/shard_map/reduce_scatter | solution.py:69
  610.3 1.8 convolution_bitcast_fusion
  612.1 1.8 convolution_convert_fusion
  613.9 250.7 %all-reduce.2.cloned.1.call-done = f32[256,256]{0,1:T(8,128)} async-done(((f32[256,256]{0,1:T(8,128)}), f32[256,256]{0,1:T(8,128)}) %all-reduce.2.cloned.1.call-update) | async-done | bytes 262160 | tf_op jit(solution)/shard_map/psum | solution.py:79
  864.6 1.0 broadcast_multiply_fusion.2
  865.5 0.8 copy.12
  (47 shorter events, 5.3 us)
Async XLA Ops:
  7.2 0.9 copy-start
  7.2 66.0 %all-gather.3.cloned.1.call-start = ((), (), s32[]{:S(2)}) async-start(), calls=%async_computation.2 | async-start | bytes 2228224 | tf_op jit(solution)/shard_map/all_gather | solution.py:55
  9.8 293.8 %reduce-scatter.3.cloned.1.call-start = ((), (), s32[]{:S(2)}) async-start(), calls=%async_computation.3 | async-start | bytes 2228224 | tf_op jit(solution)/shard_map/reduce_scatter | solution.py:59
  73.2 2.4 copy-start.2
  241.2 62.4 %copy-start.4 = (bf16[256,256]{1,0:T(8,128)(2,1)S(1)}, bf16[256,256]{1,0:T(8,128)(2,1)}, u32[]{:S(2)}) copy-start(bf16[256,256]{1,0:T(8,128)(2,1)} %param.17) | copy-start | bytes 393220
  245.0 102.6 %all-gather.5.cloned.1.call-start = ((), (), s32[]{:S(2)}) async-start(), calls=%async_computation.4 | async-start | bytes 2228224 | tf_op jit(solution)/shard_map/all_gather | solution.py:65
  305.4 304.8 %reduce-scatter.5.cloned.1.call-start = ((), (), s32[]{:S(2)}) async-start(), calls=%async_computation.5 | async-start | bytes 2228224 | tf_op jit(solution)/shard_map/reduce_scatter | solution.py:69
  347.6 2.5 copy-start.1
  517.5 94.7 %copy-start.3 = (bf16[256,256]{1,0:T(8,128)(2,1)S(1)}, bf16[256,256]{1,0:T(8,128)(2,1)}, u32[]{:S(2)}) copy-start(bf16[256,256]{1,0:T(8,128)(2,1)} %param.12) | copy-start | bytes 393220
  521.3 343.2 %all-reduce.2.cloned.1.call-start = ((), (), s32[]{:S(2)}) async-start(), calls=%async_computation.6 | async-start | bytes 524288 | tf_op jit(solution)/shard_map/psum | solution.py:79
Sparse Core Ops, SparseCore 0:
  11.0 62.1 all-gather.2
  245.2 58.3 reduce-scatter.2
  306.0 41.5 all-gather.4
  521.5 88.7 reduce-scatter.4
  617.0 247.4 all-reduce.1
where the time goes:
time: 875 us; the launch traced here: 873 us
  waiting for transfers between devices  488 us (56%)
  other arithmetic  218 us (25%)
  matrix products  78.6 us (9%)
  local copies, waits for them, and re-layouts  54.7 us (6%)
  loops' own time  19.5 us (2%)
  between operations  13.8 us (2%)
    psum x1, waiting for transfers between devices, on_device(): lax.psum(local_weight, ('row', 'col')) * (1.0 / math.sqrt(node_total))  251 us
    scatter-add x10, other arithmetic, one_block(): running_sum.at[put_index].add(products * live_slots[:, None, None])  193 us
    reduce_scatter x1, waiting for transfers between devices, on_device(): lax.psum_scatter(partial_back.astype(jnp.bfloat16), 'row', scatter_dimens...  88.9 us
    all_gather x1, waiting for transfers between devices, on_device(): gathered = lax.all_gather(projected, 'row', axis=0, tiled=True)  61.9 us
    reduce_scatter x1, waiting for transfers between devices, on_device(): lax.psum_scatter(partial_value.astype(jnp.bfloat16), 'col', scatter_dimen...  58.5 us
    dot_general x5, matrix products, one_block(): jnp.einsum('kab,kaf->kbf', block_values, picked, preferred_element_type=j...  36.9 us
    dot_general x5, matrix products, one_block(): jnp.einsum('kab,kbf->kaf', block_values, picked, preferred_element_type=j...  36.4 us
    gather x10, local copies, waits for them, and re-layouts, one_block(): picked = source_tiles[take_index]  27.9 us
  transfers between devices with their start and end apart: 5, of which 5 were waited for; matrix products, arithmetic and copies ran while one was open for 2% of the time, Pallas kernels for 0%

commit v1 on v0

v1 whole, which is shorter than its diff:
```python
import functools
import math

import jax
import jax.numpy as jnp
from jax import lax
from jax.experimental import pallas as pl
from jax.experimental.pallas import tpu as pltpu
from jax.sharding import Mesh, PartitionSpec as P


def gelu_tanh(value):
    return jax.nn.gelu(value, approximate=True)


def tile_kernel(count_ref, put_ref, take_ref, tiles_ref, source_ref, out_ref, sum_ref, *, unroll, transpose):
    step = pl.program_id(0)
    group, size, _ = tiles_ref.shape
    spare = sum_ref.shape[0] // size - 1
    live = count_ref[0]
    first = step * group
    contract = (((0,), (0,)), ((), ())) if transpose else (((1,), (0,)), ((), ()))

    @pl.when(step == 0)
    def _():
        sum_ref[...] = jnp.zeros_like(sum_ref)

    def batch(index, carry):
        rows, products = [], []
        for lane in range(unroll):
            place = index * unroll + lane
            slot = first + place
            used = slot < live
            put = jnp.where(used, put_ref[slot], spare)
            take = jnp.where(used, take_ref[slot], 0)
            picked = source_ref[pl.ds(pl.multiple_of(take * size, size), size), :]
            rows.append(pl.multiple_of(put * size, size))
            products.append(
                lax.dot_general(tiles_ref[place], picked, contract, preferred_element_type=jnp.float32)
            )
        for row, product in zip(rows, products):
            sum_ref[pl.ds(row, size), :] += product
        return carry

    todo = jnp.clip(live - first, 0, group)
    lax.fori_loop(0, (todo + unroll - 1) // unroll, batch, 0)

    @pl.when(step == pl.num_programs(0) - 1)
    def _():
        out_ref[...] = sum_ref[pl.ds(0, out_ref.shape[0]), :].astype(out_ref.dtype)


def tile_products(live_count, put_ids, take_ids, block_tiles, source, out_rows, transpose):
    slots, size, _ = block_tiles.shape
    width = source.shape[1]
    group = math.gcd(slots, 32)
    unroll = math.gcd(group, 16)
    return pl.pallas_call(
        functools.partial(tile_kernel, unroll=unroll, transpose=transpose),
        out_shape=jax.ShapeDtypeStruct((out_rows, width), jnp.bfloat16),
        grid_spec=pltpu.PrefetchScalarGridSpec(
            num_scalar_prefetch=3,
            grid=(slots // group,),
            in_specs=[
                pl.BlockSpec(
                    (group, size, size),
                    lambda i, count, put, take: (jnp.minimum(i, jnp.maximum(count[0] - 1, 0) // group), 0, 0),
                ),
                pl.BlockSpec(source.shape, lambda i, *_: (0, 0), pipeline_mode=pl.Buffered(1)),
            ],
            out_specs=pl.BlockSpec((out_rows, width), lambda i, *_: (0, 0)),
            scratch_shapes=[pltpu.VMEM((out_rows + size, width), jnp.float32)],
        ),
        compiler_params=pltpu.CompilerParams(vmem_limit_bytes=40 << 20),
        cost_estimate=pl.CostEstimate(
            flops=2 * slots * size * size * width,
            bytes_accessed=2 * slots * size * size + 4 * out_rows * width,
            transcendentals=0,
        ),
    )(live_count, put_ids, take_ids, block_tiles, source)


def scatter_sum(parts, axes):
    devices = lax.axis_size(axes)
    chunks = parts.reshape(devices, parts.shape[0] // devices, parts.shape[1])
    received = lax.all_to_all(chunks, axes, 0, 0)
    return received.astype(jnp.float32).sum(0)


def on_device(row, col, features, weight, tile_rows, tile_cols, tile_count, tile_values, grad_out):
    seg_rows, feat_width = features.shape
    block_tiles = tile_values[0, 0]
    tile_row_ids = tile_rows[0, 0]
    tile_col_ids = tile_cols[0, 0]
    live_count = tile_count[0]
    row_span = lax.axis_size(col) * seg_rows
    col_span = lax.axis_size(row) * seg_rows
    node_total = seg_rows * lax.axis_size(row) * lax.axis_size(col)

    gathered = features
    for axis in reversed(row):
        gathered = lax.all_gather(gathered, axis, axis=0, tiled=True)
    partial_value = tile_products(
        live_count, tile_row_ids, tile_col_ids, block_tiles, gathered, row_span, False
    )
    aggregated = scatter_sum(partial_value, col).astype(jnp.bfloat16)
    summed = jnp.dot(aggregated, weight, preferred_element_type=jnp.float32)
    activations, pullback = jax.vjp(gelu_tanh, summed)
    gradient = pullback(grad_out.astype(jnp.float32))[0].astype(jnp.bfloat16)
    activations = activations.astype(jnp.bfloat16)
    grad_blocks = lax.all_gather(gradient, col, axis=0, tiled=True)

    local_weight = lax.dot_general(
        aggregated, gradient, (((0,), (0,)), ((), ())), preferred_element_type=jnp.float32
    )
    weight_slice = scatter_sum(local_weight, col)
    weight_slices = lax.all_gather(weight_slice, row, axis=0)
    weight_slice = weight_slices.sum(0) * (1.0 / math.sqrt(node_total))
    weight_grad = lax.all_gather(weight_slice, col, axis=0, tiled=True)

    partial_back = tile_products(
        live_count, tile_col_ids, tile_row_ids, block_tiles, grad_blocks, col_span, True
    )
    back_sum = scatter_sum(partial_back, row).astype(jnp.bfloat16)
    feature_grad = lax.dot_general(
        back_sum, weight, (((1,), (1,)), ((), ())), preferred_element_type=jnp.float32
    ).astype(jnp.bfloat16)
    return (activations, feature_grad, weight_grad)


def solution(mesh):
    row, col = ("row_far", "row_near"), ("col_far", "col_mid", "col_near")
    split = Mesh(mesh.devices.reshape(4, 4, 4, 2, 2), row + col)
    by_row, by_col = P(row + col, None), P(col + row, None)
    placed = (
        by_col,
        P(),
        P(row, col, None),
        P(row, col, None),
        P(row, col),
        P(row, col, None, None, None),
        by_row,
    )
    return jax.shard_map(
        functools.partial(on_device, row, col),
        mesh=split,
        in_specs=placed,
        out_specs=(by_row, by_col, P()),
        check_vma=False,
    )
```

time: 875 us -> 280 us (0.32)
  waiting for transfers between devices: 488 us -> 61.9 us
  other arithmetic: 218 us -> 2.03 us
  blocking collectives: 0 us -> 161 us
  matrix products: 78.6 us -> 3.74 us
  local copies, waits for them, and re-layouts: 54.7 us -> 4.6 us
  loops' own time: 19.5 us -> 0 us
  starting transfers between devices: 0.21 us -> 19 us
  Pallas kernels: 0 us -> 9.85 us
    psum x1 -> x0, waiting for transfers between devices: 251 us -> none  [on_device(): lax.psum(local_weight, ('row', 'col')) * (1.0 / math.sqrt(node_total))]
    scatter-add x10 -> x0, other arithmetic: 193 us -> none  [one_block(): running_sum.at[put_index].add(products * live_slots[:, None, None])]
    reduce_scatter x2 -> x0, waiting for transfers between devices: 147 us -> none  [the longest x1 88.9 us: on_device(): lax.psum_scatter(partial_back.astype(jnp.bfloat16), 'row', scatter_dimens...]
    all_gather x0 -> x3, blocking collectives: none -> 126 us  [the longest x1 79.3 us: on_device(): weight_slices = lax.all_gather(weight_slice, row, axis=0)]
    dot_general x12 -> x2, matrix products: 76.9 us -> 2.86 us  [the longest x1 1.8 us: on_device(): lax.dot_general(aggregated, gradient, (((0,), (0,)), ((), ())), preferred...]
    all_to_all x0 -> x1, blocking collectives: none -> 35.1 us  [scatter_sum(): received = lax.all_to_all(chunks, axes, 0, 0)]
    gather x10 -> x0, local copies, waits for them, and re-layouts: 27.9 us -> none  [one_block(): picked = source_tiles[take_index]]
    all_gather x2, waiting for transfers between devices: 89.6 us -> 61.9 us  [the longest x1 31.3 us: on_device(): gathered = lax.all_gather(gathered, axis, axis=0, tiled=True)]
  transfers between devices with their start and end apart: 5 -> 4, of which waited for: 5 -> 2; matrix products, arithmetic and copies ran while one was open for 2% -> 1% of each run, Pallas kernels for 0% -> 2%
where the time goes in v1:
time: 280 us; the launch traced here: 277 us
  blocking collectives  161 us (58%)
  waiting for transfers between devices  61.9 us (22%)
  starting transfers between devices  19 us (7%)
  between operations  14.8 us (5%)
  Pallas kernels  9.85 us (4%)
  local copies, waits for them, and re-layouts  4.6 us (2%)
  matrix products  3.74 us (1%)
    all_gather x1, blocking collectives, on_device(): weight_slices = lax.all_gather(weight_slice, row, axis=0)  79.3 us
    all_to_all x1, blocking collectives, scatter_sum(): received = lax.all_to_all(chunks, axes, 0, 0)  35.1 us
    all_gather x1, waiting for transfers between devices, on_device(): gathered = lax.all_gather(gathered, axis, axis=0, tiled=True)  31.3 us
    all_gather x1, waiting for transfers between devices, on_device(): grad_blocks = lax.all_gather(gradient, col, axis=0, tiled=True)  30.6 us
    all_gather x1, blocking collectives, on_device(): weight_grad = lax.all_gather(weight_slice, col, axis=0, tiled=True)  25.9 us
    all_gather x1, blocking collectives, on_device(): gathered = lax.all_gather(gathered, axis, axis=0, tiled=True)  20.6 us
    all_to_all x2, starting transfers between devices, scatter_sum(): received = lax.all_to_all(chunks, axes, 0, 0)  18.9 us
    pallas_call x2, Pallas kernels, tile_products(): pl.pallas_call(functools.partial(tile_kernel, unroll=unroll, transpose=tr...  9.85 us
  transfers between devices with their start and end apart: 4, of which 2 were waited for; matrix products, arithmetic and copies ran while one was open for 1% of the time, Pallas kernels for 2%

profile of v1, /device:TPU:2, one launch (start us, length us, event | category | flops | bytes accessed | tf_op | source)
XLA Modules:
  0.0 276.8 jit_solution(16690599144195848225)
XLA Ops:
  7.2 0.0 copy-start
  7.2 0.0 all-gather.4.cloned.1.call-start
  7.2 20.6 %all_gather.18 = bf16[1024,256]{1,0:T(8,128)(2,1)} all-gather(bf16[256,256]{1,0:T(8,128)(2,1)} %param.7), channel_id=1, replica_groups=mesh['row_far'=4,'row_near'=4,'col_far'=4,'col_mid'=2,'col_near'=2] {'ro..., dimensions={0}, use_global_device_ids=true | all-gather | bytes 655360 | tf_op jit(solution)/shard_map/all_gather | solution.py:102
  27.8 0.0 all-gather.4.cloned.1.call-update
  27.8 0.0 all-gather.6.cloned.1.call-start
  28.5 0.7 reduce.2.put_ref.take_ref
  29.2 0.7 reduce.3.take_ref.put_ref
  29.9 31.3 %all-gather.4.cloned.1.call-done.source_ref = bf16[4096,256]{1,0:T(8,128)(2,1)} async-done(((bf16[1024,256]{1,0:T(8,128)(2,1)}), bf16[4096,256]{1,0:T(8,128)(2,1)}) %all-gather.4.cloned.1.call-update) | async-done | bytes 2097168 | tf_op jit(solution)/shard_map/all_gather | solution.py:102
  61.2 0.0 copy-start.2
  61.2 1.6 copy-done.2
  62.8 4.2 %shard_map.94 = bf16[4096,256]{1,0:T(8,128)(2,1)S(1)} custom-call(s32[1]{0:T(128)} %bitcast.15.count_ref, s32[320]{0:T(512)S(1)} %reduce.2.put_ref.take_ref, s32[320]{0:T(512)S(1)} %reduce.3.take_ref.put_ref, bf16[320,128,128]{2,1,0:T(8,128)(2,1)} %bitcast.18, bf16[4096,256]{1,0:T(8,128)(2,1)S(1)} %copy-done.2), custom_call_target="tpu_custom_call" | custom-call | flops 2684354560 | bytes 14680064 | tf_op jit(solution)/shard_map/pallas_call | solution.py:58
  67.0 35.1 %all_to_all.15 = bf16[16,256,256]{2,1,0:T(8,128)(2,1)S(1)} all-to-all(bf16[16,256,256]{2,1,0:T(8,128)(2,1)S(1)} %bitcast.17), channel_id=1, replica_groups=mesh['row_far'=4,'row_near'=4,'col_far'=4,'col_mid'=2,'col_near'=2] {'co..., dimensions={0} | all-to-all | bytes 4194304 | tf_op jit(solution)/shard_map/all_to_all | solution.py:86
  102.1 0.0 copy-start.3
  102.1 0.3 reduce_sum.42
  102.4 0.0 copy-done
  102.4 0.6 copy-done.3
  103.0 1.1 fusion.2
  104.0 0.0 all-gather.6.cloned.1.call-update
  104.1 0.1 copy.12
  104.2 1.8 fusion.10
  106.0 6.0 %all-to-all-start.2 = ((f32[16,16,256]{2,1,0:T(8,128)}), f32[16,16,256]{2,1,0:T(8,128)S(1)}, u32[]{:S(2)}, u32[]{:S(2)}) async-start(f32[16,16,256]{2,1,0:T(8,128)} %fusion.10), calls=%async_computation.2 | async-start | bytes 524288 | tf_op jit(solution)/shard_map/all_to_all | solution.py:86
  112.0 30.6 %all-gather.6.cloned.1.call-done.source_ref = bf16[4096,256]{1,0:T(8,128)(2,1)} async-done(((bf16[256,256]{1,0:T(8,128)(2,1)}), bf16[4096,256]{1,0:T(8,128)(2,1)}) %all-gather.6.cloned.1.call-update) | async-done | bytes 2097168 | tf_op jit(solution)/shard_map/all_gather | solution.py:111
  142.6 0.0 copy-start.1
  142.6 1.6 copy-done.1
  144.2 5.7 %shard_map.95 = bf16[4096,256]{1,0:T(8,128)(2,1)} custom-call(s32[1]{0:T(128)} %bitcast.16.count_ref, s32[320]{0:T(512)S(1)} %reduce.3.take_ref.put_ref, s32[320]{0:T(512)S(1)} %reduce.2.put_ref.take_ref, bf16[320,128,128]{2,1,0:T(8,128)(2,1)} %bitcast.19, bf16[4096,256]{1,0:T(8,128)(2,1)S(1)} %copy-done.1), custom_call_target="tpu_custom_call" | custom-call | flops 2684354560 | bytes 14680064 | tf_op jit(solution)/shard_map/pallas_call | solution.py:58
  149.9 0.0 all-to-all-done.2
  149.9 12.9 %all-to-all-start.1 = ((bf16[16,256,256]{2,1,0:T(8,128)(2,1)}), bf16[16,256,256]{2,1,0:T(8,128)(2,1)S(1)}, u32[]{:S(2)}, u32[]{:S(2)}) async-start(bf16[16,256,256]{2,1,0:T(8,128)(2,1)} %bitcast.3), calls=%async_computation.1 | async-start | bytes 4194304 | tf_op jit(solution)/shard_map/all_to_all | solution.py:86
  162.8 79.3 %all-gather = f32[256,256]{1,0:T(8,128)S(1)} all-gather(f32[16,256]{1,0:T(8,128)S(1)} %reduce_sum.44), channel_id=2, replica_groups=mesh['row_far'=4,'row_near'=4,'col_far'=4,'col_mid'=2,'col_near'=2] {'ro..., dimensions={0}, use_global_device_ids=true | all-gather | bytes 278528 | tf_op jit(solution)/shard_map/all_gather | solution.py:117
  242.1 25.9 %all_gather.23 = f32[256,256]{1,0:T(8,128)S(1)} all-gather(f32[16,256]{1,0:T(8,128)S(1)} %broadcast_multiply_fusion), channel_id=1, replica_groups=mesh['row_far'=4,'row_near'=4,'col_far'=4,'col_mid'=2,'col_near'=2] {'co..., dimensions={0}, use_global_device_ids=true | all-gather | bytes 278528 | tf_op jit(solution)/shard_map/all_gather | solution.py:119
  268.0 0.0 all-to-all-done.1
  268.0 0.3 reduce_sum.43
  268.3 0.9 convolution_convert_fusion
  269.2 0.7 copy.15
  (3 shorter events, 0.0 us)
Async XLA Ops:
  7.2 95.2 %copy-start = (bf16[256,256]{1,0:T(8,128)(2,1)S(1)}, bf16[256,256]{1,0:T(8,128)(2,1)}, u32[]{:S(2)}) copy-start(bf16[256,256]{1,0:T(8,128)(2,1)} %param.8) | copy-start | bytes 393220
  7.2 54.0 %all-gather.4.cloned.1.call-start = ((), (), s32[]{:S(2)}) async-start(), calls=%async_computation.3 | async-start | bytes 2621440 | tf_op jit(solution)/shard_map/all_gather | solution.py:102
  27.8 114.8 %all-gather.6.cloned.1.call-start = ((), (), s32[]{:S(2)}) async-start(), calls=%async_computation.4 | async-start | bytes 2228224 | tf_op jit(solution)/shard_map/all_gather | solution.py:111
  61.2 1.6 copy-start.2
  102.1 0.9 copy-start.3
  106.0 43.9 %all-to-all-start.2 = ((f32[16,16,256]{2,1,0:T(8,128)}), f32[16,16,256]{2,1,0:T(8,128)S(1)}, u32[]{:S(2)}, u32[]{:S(2)}) async-start(f32[16,16,256]{2,1,0:T(8,128)} %fusion.10), calls=%async_computation.2 | async-start | bytes 524288 | tf_op jit(solution)/shard_map/all_to_all | solution.py:86
  142.6 1.6 copy-start.1
  149.9 118.2 %all-to-all-start.1 = ((bf16[16,256,256]{2,1,0:T(8,128)(2,1)}), bf16[16,256,256]{2,1,0:T(8,128)(2,1)S(1)}, u32[]{:S(2)}, u32[]{:S(2)}) async-start(bf16[16,256,256]{2,1,0:T(8,128)(2,1)} %bitcast.3), calls=%async_computation.1 | async-start | bytes 4194304 | tf_op jit(solution)/shard_map/all_to_all | solution.py:86
Sparse Core Ops, SparseCore 0:
  27.9 33.2 all-gather.3
  104.2 38.3 all-gather.5

commit v2 on v1

v2 whole, which is shorter than its diff:
```python
import functools
import math

import jax
import jax.numpy as jnp
from jax import lax
from jax.experimental import pallas as pl
from jax.experimental.pallas import tpu as pltpu
from jax.sharding import Mesh, PartitionSpec as P

def gelu_tanh(value):
    return jax.nn.gelu(value, approximate=True)


def tile_kernel(count_ref, put_ref, take_ref, tiles_ref, *refs, pieces, outs, unroll, transpose):
    piece_refs, out_refs = refs[: len(pieces)], refs[len(pieces) : len(pieces) + outs]
    source_ref, sum_ref, arrived = refs[len(pieces) + outs :]
    step = pl.program_id(0)
    group, size, _ = tiles_ref.shape
    spare = sum_ref.shape[0] // size - 1
    live = count_ref[0]
    first = step * group
    contract = (((0,), (0,)), ((), ())) if transpose else (((1,), (0,)), ((), ()))

    @pl.when(step == 0)
    def _():
        copies, at = [], 0
        for piece, (blocks, rows) in zip(piece_refs, pieces):
            for block in range(blocks):
                copies.append(
                    pltpu.make_async_copy(
                        piece.at[block, pl.ds(0, rows), :],
                        source_ref.at[pl.ds(at, rows), :],
                        arrived.at[len(copies)],
                    )
                )
                at += rows
        for copy in copies:
            copy.start()
        sum_ref[...] = jnp.zeros_like(sum_ref)
        for copy in copies:
            copy.wait()

    def batch(index, carry):
        rows, products = [], []
        for lane in range(unroll):
            place = index * unroll + lane
            slot = first + place
            used = slot < live
            put = jnp.where(used, put_ref[slot], spare)
            take = jnp.where(used, take_ref[slot], 0)
            picked = source_ref[pl.ds(pl.multiple_of(take * size, size), size), :]
            rows.append(pl.multiple_of(put * size, size))
            products.append(
                lax.dot_general(tiles_ref[place], picked, contract, preferred_element_type=jnp.float32)
            )
        for row, product in zip(rows, products):
            sum_ref[pl.ds(row, size), :] += product
        return carry

    todo = jnp.clip(live - first, 0, group)
    lax.fori_loop(0, (todo + unroll - 1) // unroll, batch, 0)

    @pl.when(step == pl.num_programs(0) - 1)
    def _():
        at = 0
        for out in out_refs:
            out[...] = sum_ref[pl.ds(at, out.shape[0]), :].astype(out.dtype)
            at += out.shape[0]


def tile_products(live_count, put_ids, take_ids, block_tiles, sources, rows_used, outs, transpose):
    slots, size, _ = block_tiles.shape
    width = sources[0].shape[-1]
    sources = [source.reshape((-1,) + source.shape[-2:]) for source in sources]
    pieces = [(source.shape[0], rows_used or source.shape[1]) for source in sources]
    source_rows = sum(blocks * rows for blocks, rows in pieces)
    sum_rows = sum(rows for rows, _ in outs)
    group = math.gcd(slots, 32)
    unroll = math.gcd(group, 16)
    whole = lambda i, *_: (0, 0)
    return pl.pallas_call(
        functools.partial(
            tile_kernel, pieces=pieces, outs=len(outs), unroll=unroll, transpose=transpose
        ),
        out_shape=[jax.ShapeDtypeStruct((rows, width), kind) for rows, kind in outs],
        grid_spec=pltpu.PrefetchScalarGridSpec(
            num_scalar_prefetch=3,
            grid=(slots // group,),
            in_specs=[
                pl.BlockSpec(
                    (group, size, size),
                    lambda i, count, put, take: (jnp.minimum(i, jnp.maximum(count[0] - 1, 0) // group), 0, 0),
                )
            ]
            + [pl.BlockSpec(memory_space=pl.ANY)] * len(pieces),
            out_specs=[pl.BlockSpec((rows, width), whole) for rows, _ in outs],
            scratch_shapes=[
                pltpu.VMEM((source_rows, width), jnp.bfloat16),
                pltpu.VMEM((sum_rows + size, width), jnp.float32),
                pltpu.SemaphoreType.DMA((sum(blocks for blocks, _ in pieces),)),
            ],
        ),
        compiler_params=pltpu.CompilerParams(vmem_limit_bytes=56 << 20),
        cost_estimate=pl.CostEstimate(
            flops=8 * slots * size * size * width,
            bytes_accessed=2 * slots * size * size + 4 * sum_rows * width,
            transcendentals=0,
        ),
    )(live_count, put_ids, take_ids, block_tiles, *sources)


def exchange(chunks, axes):
    return lax.all_to_all(chunks, axes, 0, 0)


def spread(block, axes):
    devices = lax.axis_size(axes)
    return exchange(lax.optimization_barrier(jnp.broadcast_to(block[None], (devices,) + block.shape)), axes)


def total(parts):
    return parts.astype(jnp.float32).sum(0)


def shift(block, axis, by):
    devices = lax.axis_size(axis)
    return lax.ppermute(block, axis, [(k, (k + by) % devices) for k in range(devices)])


def on_device(features, weight, tile_rows, tile_cols, tile_count, tile_values, grad_out):
    seg_rows, feat_width = features.shape
    block_tiles = tile_values[0, 0]
    size = block_tiles.shape[-1]
    live_count = tile_count[0]
    tile_row_ids = tile_rows[0, 0]
    tile_col_ids = tile_cols[0, 0]
    far, near = lax.axis_size("row_far"), lax.axis_size("row_near")
    mid = lax.axis_size(("col_far", "col_mid"))
    row, col = ("row_far", "row_near"), ("col_far", "col_mid", "col_near")
    node_total = seg_rows * lax.axis_size(row) * lax.axis_size(col)
    seg_tiles = seg_rows // size
    far_rows, mid_rows = near * seg_rows, mid * seg_rows
    far_tiles = near * seg_tiles
    half_tiles, half_rows = far_tiles // 2, far_rows // 2

    away = (tile_col_ids // far_tiles - lax.axis_index("row_far")) % far
    inner = tile_col_ids % far_tiles
    upper = inner >= half_tiles
    col_take = jnp.where(away == 0, 0, jnp.where(away == 3, 1, away + 1)) * far_tiles + inner
    col_put = (
        jnp.where(
            away == 0,
            0,
            jnp.where(
                away == 1,
                jnp.where(upper, 1 * far_tiles, 3 * far_tiles),
                jnp.where(
                    away == 2,
                    jnp.where(upper, 2 * far_tiles, 1 * far_tiles),
                    jnp.where(upper, 3 * far_tiles, 2 * far_tiles),
                ),
            ),
        )
        + inner
    )
    other = (tile_row_ids // seg_tiles) % 2 != lax.axis_index("col_near")
    row_place = (
        other.astype(jnp.int32) * (mid * seg_tiles)
        + tile_row_ids // (2 * seg_tiles) * seg_tiles
        + tile_row_ids % seg_tiles
    )

    own = lax.all_gather(features, "row_near", axis=0, tiled=True)
    left, right = shift(own, "row_far", 1), shift(own, "row_far", -1)
    low, high = shift(left[:half_rows], "row_far", 1), shift(right[half_rows:], "row_far", -1)
    keep, send = tile_products(
        live_count, row_place, col_take, block_tiles, [own, left, right, low, high], None,
        [(mid_rows, jnp.float32), (mid_rows, jnp.bfloat16)], False,
    )
    paired = (keep + shift(send, "col_near", 1).astype(jnp.float32)).astype(jnp.bfloat16)
    parts = exchange(paired.reshape(mid, seg_rows, feat_width), ("col_far", "col_mid"))
    aggregated = total(parts).astype(jnp.bfloat16)

    summed = jnp.dot(aggregated, weight, preferred_element_type=jnp.float32)
    activations, pullback = jax.vjp(gelu_tanh, summed)
    gradient = pullback(grad_out.astype(jnp.float32))[0].astype(jnp.bfloat16)
    activations = activations.astype(jnp.bfloat16)

    local_weight = lax.dot_general(
        aggregated, gradient, (((0,), (0,)), ((), ())), preferred_element_type=jnp.float32
    ).astype(jnp.bfloat16)
    load = jnp.concatenate(
        [
            jnp.broadcast_to(gradient[None], (mid,) + gradient.shape),
            local_weight.reshape(mid, -1, feat_width),
        ],
        axis=1,
    )
    mine = exchange(load, ("col_far", "col_mid"))
    theirs = shift(mine, "col_near", 1)
    weight_pair = total(mine[:, seg_rows:]) + total(theirs[:, seg_rows:])
    weight_rows = feat_width // lax.axis_size(col)
    weight_slice = lax.dynamic_slice_in_dim(weight_pair, lax.axis_index("col_near") * weight_rows, weight_rows, 0)
    weight_slices = jnp.broadcast_to(weight_slice[None], (lax.axis_size(row),) + weight_slice.shape)
    mine, theirs, weight_slices = lax.optimization_barrier((mine, theirs, weight_slices))
    weight_slices = exchange(weight_slices, row)

    own, right_one, left_one, right_two, left_two = tile_products(
        live_count, col_put, row_place, block_tiles, [mine, theirs], seg_rows,
        [
            (far_rows, jnp.float32),
            (far_rows, jnp.bfloat16),
            (far_rows, jnp.bfloat16),
            (half_rows, jnp.float32),
            (half_rows, jnp.float32),
        ],
        True,
    )
    right_one, left_one, weight_slices = lax.optimization_barrier((right_one, left_one, weight_slices))
    from_left, from_right = shift(right_one, "row_far", 1), shift(left_one, "row_far", -1)
    weight_slice = total(weight_slices) * (1.0 / math.sqrt(node_total))
    weight_grad = spread(weight_slice, col).reshape(feat_width, feat_width)
    from_left, from_right, weight_grad = lax.optimization_barrier((from_left, from_right, weight_grad))
    right_two = (right_two + from_left[:half_rows].astype(jnp.float32)).astype(jnp.bfloat16)
    left_two = (left_two + from_right[half_rows:].astype(jnp.float32)).astype(jnp.bfloat16)
    low, high = shift(right_two, "row_far", 1), shift(left_two, "row_far", -1)
    low = own[:half_rows] + low.astype(jnp.float32) + from_right[:half_rows].astype(jnp.float32)
    high = own[half_rows:] + high.astype(jnp.float32) + from_left[half_rows:].astype(jnp.float32)
    mixed = jnp.concatenate([low, high], axis=0).astype(jnp.bfloat16)
    parts = exchange(mixed.reshape(near, seg_rows, feat_width), "row_near")
    back_sum = total(parts).astype(jnp.bfloat16)

    feature_grad = lax.dot_general(
        back_sum, weight, (((1,), (1,)), ((), ())), preferred_element_type=jnp.float32
    ).astype(jnp.bfloat16)
    return (activations, feature_grad, weight_grad)


def solution(mesh):
    row, col = ("row_far", "row_near"), ("col_far", "col_mid", "col_near")
    split = Mesh(mesh.devices.reshape(4, 4, 4, 2, 2), row + col)
    by_row, by_col = P(row + col, None), P(col + row, None)
    placed = (
        by_col,
        P(),
        P(row, col, None),
        P(row, col, None),
        P(row, col),
        P(row, col, None, None, None),
        by_row,
    )
    return jax.shard_map(
        on_device,
        mesh=split,
        in_specs=placed,
        out_specs=(by_row, by_col, P()),
        check_vma=False,
    )
```

time: 280 us -> 179 us (0.64)
  blocking collectives: 161 us -> 72.7 us
  waiting for transfers between devices: 61.9 us -> 45.1 us
  between operations: 14.8 us -> 1.54 us
  Pallas kernels: 9.85 us -> 19.1 us
  starting transfers between devices: 19 us -> 27.8 us
  other arithmetic: 2.03 us -> 6.47 us
    all_gather x3 -> x1, blocking collectives: 126 us -> 20.4 us  [on_device(): own = lax.all_gather(features, 'row_near', axis=0, tiled=True)]
    all_gather x2 -> x0, waiting for transfers between devices: 61.9 us -> none  [the longest x1 31.3 us: on_device(): gathered = lax.all_gather(gathered, axis, axis=0, tiled=True)]
    ppermute x0 -> x10, waiting for transfers between devices: none -> 25.8 us  [shift(): lax.ppermute(block, axis, [(k, (k + by) % devices) for k in range(devices)])]
    all_to_all x2, waiting for transfers between devices: 0.01 us -> 19.3 us  [exchange(): return lax.all_to_all(chunks, axes, 0, 0)]
    all_to_all x1 -> x3, blocking collectives: 35.1 us -> 52.3 us  [exchange(): return lax.all_to_all(chunks, axes, 0, 0)]
    ppermute x0 -> x10, starting transfers between devices: none -> 14.9 us  [shift(): lax.ppermute(block, axis, [(k, (k + by) % devices) for k in range(devices)])]
    pallas_call x2, Pallas kernels: 9.85 us -> 19.1 us  [tile_products(): pl.pallas_call(functools.partial(tile_kernel, pieces=pieces, outs=len(out...]
    all_to_all x2, starting transfers between devices: 18.9 us -> 12.9 us  [exchange(): return lax.all_to_all(chunks, axes, 0, 0)]
  transfers between devices with their start and end apart: 4 -> 12, of which waited for: 2 -> 9; matrix products, arithmetic and copies ran while one was open for 1% -> 1% of each run, Pallas kernels for 2% -> 5%
where the time goes in v2:
time: 179 us; the launch traced here: 177 us
  blocking collectives  72.7 us (41%)
  waiting for transfers between devices  45.1 us (25%)
  starting transfers between devices  27.8 us (16%)
  Pallas kernels  19.1 us (11%)
  other arithmetic  6.47 us (4%)
  local copies, waits for them, and re-layouts  2.42 us (1%)
  matrix products  2.12 us (1%)
    all_to_all x3, blocking collectives, exchange(): return lax.all_to_all(chunks, axes, 0, 0)  52.3 us
    ppermute x10, waiting for transfers between devices, shift(): lax.ppermute(block, axis, [(k, (k + by) % devices) for k in range(devices)])  25.8 us
    all_gather x1, blocking collectives, on_device(): own = lax.all_gather(features, 'row_near', axis=0, tiled=True)  20.4 us
    all_to_all x2, waiting for transfers between devices, exchange(): return lax.all_to_all(chunks, axes, 0, 0)  19.3 us
    pallas_call x2, Pallas kernels, tile_products(): pl.pallas_call(functools.partial(tile_kernel, pieces=pieces, outs=len(out...  19.1 us
    ppermute x10, starting transfers between devices, shift(): lax.ppermute(block, axis, [(k, (k + by) % devices) for k in range(devices)])  14.9 us
    all_to_all x2, starting transfers between devices, exchange(): return lax.all_to_all(chunks, axes, 0, 0)  12.9 us
  transfers between devices with their start and end apart: 12, of which 9 were waited for; matrix products, arithmetic and copies ran while one was open for 1% of the time, Pallas kernels for 5%

profile of v2, /device:TPU:2, one launch (start us, length us, event | category | flops | bytes accessed | tf_op | source)
XLA Modules:
  0.0 177.3 jit_solution(12480239338533180439)
XLA Ops:
  0.6 0.0 copy-start
  0.6 20.4 %all_gather.3 = bf16[1024,256]{1,0:T(8,128)(2,1)S(1)} all-gather(bf16[256,256]{1,0:T(8,128)(2,1)} %param.7), channel_id=1, replica_groups=mesh['row_far'=4,'row_near'=4,'col_far'=4,'col_mid'=2,'col_near'=2] {'ro..., dimensions={0}, use_global_device_ids=true | all-gather | bytes 655360 | tf_op jit(solution)/shard_map/all_gather | solution.py:174
  21.1 0.0 copy-start.3
  21.1 3.0 %collective-permute-start.1 = (bf16[1024,256]{1,0:T(8,128)(2,1)S(1)}, bf16[1024,256]{1,0:T(8,128)(2,1)S(1)}, u32[]{:S(2)}, u32[]{:S(2)}) collective-permute-start(bf16[1024,256]{1,0:T(8,128)(2,1)S(1)} %all_gather.3), channel_id=1, source_target_pairs={{0,192},{64,0},{128,64},{192,128},{1,193},{65,1},{129,65},{193,129... | collective-permute-start | bytes 1572872 | tf_op jit(solution)/shard_map/ppermute | solution.py:128
  24.1 0.0 collective-permute-start
  24.1 8.4 %collective-permute-done.1 = bf16[1024,256]{1,0:T(8,128)(2,1)S(1)} collective-permute-done((bf16[1024,256]{1,0:T(8,128)(2,1)S(1)}, bf16[1024,256]{1,0:T(8,128)(2,1)S(1)}, u32[]{:S(2)}, u32[]{:S(2)}) %collective-permute-start.1) | collective-permute-done | bytes 524320 | tf_op jit(solution)/shard_map/ppermute | solution.py:128
  32.5 0.0 copy-start.5
  32.5 3.7 %collective-permute-start.3 = (bf16[512,256]{1,0:T(8,128)(2,1)S(1)}, bf16[512,256]{1,0:T(8,128)(2,1)S(1)}, u32[]{:S(2)}, u32[]{:S(2)}) collective-permute-start(bf16[512,256]{1,0:T(8,128)(2,1)S(1)} %slice.41), channel_id=1, source_target_pairs={{0,192},{64,0},{128,64},{192,128},{1,193},{65,1},{129,65},{193,129... | collective-permute-start | bytes 786440 | tf_op jit(solution)/shard_map/ppermute | solution.py:128
  36.2 0.0 collective-permute-done
  36.2 0.1 collective-permute-start.2
  37.0 0.7 reduce.2
  37.7 0.7 reduce.3
  38.4 0.6 select_add_fusion
  39.0 1.1 collective-permute-done.3
  40.1 3.8 %collective-permute-done.2 = bf16[512,256]{1,0:T(8,128)(2,1)S(1)} collective-permute-done((bf16[512,256]{1,0:T(8,128)(2,1)S(1)}, bf16[512,256]{1,0:T(8,128)(2,1)S(1)}, u32[]{:S(2)}, u32[]{:S(2)}) %collective-permute-start.2) | collective-permute-done | bytes 262176 | tf_op jit(solution)/shard_map/ppermute | solution.py:128
  43.9 0.0 copy-done.3
  43.9 0.0 copy-done.5
  43.9 0.0 copy-done.6
  43.9 0.0 copy-done.8
  43.9 0.7 copy-done.9
  44.6 9.4 %shard_map.94 = (f32[2048,256]{1,0:T(8,128)}, bf16[2048,256]{1,0:T(8,128)(2,1)}) custom-call(s32[1]{0:T(128)} %bitcast.17.count_ref, s32[320]{0:T(512)} %get-tuple-element.41.put_ref.take_ref, s32[320]{0:T(512)} %get-tuple-element.40.take_ref, bf16[320,128,128]{2,1,0:T(8,128)(2,1)} %bitcast.25, bf16[1,1024,256]{2,1,0:T(8,128)(2,1)} %bitcast.22, ...), custom_call_target="tpu_custom_call" | custom-call | flops 10737418240 | bytes 14680064 | tf_op jit(solution)/shard_map/pallas_call | solution.py:82
  54.0 0.1 collective-permute-start.4
  54.0 2.9 %collective-permute-done.4 = bf16[2048,256]{1,0:T(8,128)(2,1)S(1)} collective-permute-done((bf16[2048,256]{1,0:T(8,128)(2,1)}, bf16[2048,256]{1,0:T(8,128)(2,1)S(1)}, u32[]{:S(2)}, u32[]{:S(2)}) %collective-permute-start.4) | collective-permute-done | bytes 1048608 | tf_op jit(solution)/shard_map/ppermute | solution.py:128
  56.9 1.9 %add_convert_fusion = bf16[2048,256]{1,0:T(8,128)(2,1)S(1)} fusion(f32[2048,256]{1,0:T(8,128)} %get-tuple-element.19, bf16[2048,256]{1,0:T(8,128)(2,1)S(1)} %collective-permute-done.4), kind=kLoop, calls=%fused_computation | loop fusion | flops 1572864 | bytes 4194304 | tf_op jit(solution)/shard_map/convert_element_type | solution.py:181
  58.8 0.0 copy-start.10
  58.8 23.6 %all_to_all.25 = bf16[8,256,256]{2,1,0:T(8,128)(2,1)S(1)} all-to-all(bf16[8,256,256]{2,1,0:T(8,128)(2,1)S(1)} %bitcast.19), channel_id=1, replica_groups=mesh['row_far'=4,'row_near'=4,'col_far'=4,'col_mid'=2,'col_near'=2] {'co..., dimensions={0} | all-to-all | bytes 2097152 | tf_op jit(solution)/shard_map/all_to_all | solution.py:114
  82.4 0.1 reduce_sum.51
  82.6 0.0 copy-done
  82.6 0.0 copy-done.10
  82.6 1.0 fusion.2
  83.6 0.2 convolution_convert_fusion.1
  83.8 0.1 broadcast_in_dim.34
  83.9 0.1 pad_maximum_fusion
  84.0 19.4 %all_to_all.26.refs_0_ = bf16[8,288,256]{2,1,0:T(8,128)(2,1)S(1)} all-to-all(bf16[8,288,256]{2,1,0:T(8,128)(2,1)S(1)} %pad_maximum_fusion), channel_id=1, replica_groups=mesh['row_far'=4,'row_near'=4,'col_far'=4,'col_mid'=2,'col_near'=2] {'co..., dimensions={0} | all-to-all | bytes 2359296 | tf_op jit(solution)/shard_map/all_to_all | solution.py:114
  103.4 0.0 collective-permute-start.5
  103.4 2.8 %collective-permute-done.5.refs_1_ = bf16[8,288,256]{2,1,0:T(8,128)(2,1)S(1)} collective-permute-done((bf16[8,288,256]{2,1,0:T(8,128)(2,1)S(1)}, bf16[8,288,256]{2,1,0:T(8,128)(2,1)S(1)}, u32[]{:S(2)}, u32[]{:S(2)}) %collective-permute-start.5) | collective-permute-done | bytes 1179680 | tf_op jit(solution)/shard_map/ppermute | solution.py:128
  106.3 0.9 broadcast_in_dim.35
  107.2 4.9 %all-to-all-start.2 = ((f32[16,16,256]{2,1,0:T(8,128)}), f32[16,16,256]{2,1,0:T(8,128)S(1)}, u32[]{:S(2)}, u32[]{:S(2)}) async-start(f32[16,16,256]{2,1,0:T(8,128)} %broadcast_in_dim.35), calls=%async_computation.2 | async-start | bytes 524288 | tf_op jit(solution)/shard_map/all_to_all | solution.py:114
  112.0 0.0 copy-done.1
  112.0 0.0 copy-done.7
  112.1 9.7 %shard_map.95 = (f32[1024,256]{1,0:T(8,128)}, bf16[1024,256]{1,0:T(8,128)(2,1)}, bf16[1024,256]{1,0:T(8,128)(2,1)}, f32[512,256]{1,0:T(8,128)}, f32[512,256]{1,0:T(8,128)}) custom-call(s32[1]{0:T(128)} %bitcast.18.count_ref, s32[320]{0:T(512)} %get-tuple-element.39.put_ref, s32[320]{0:T(512)} %get-tuple-element.41.put_ref.take_ref, ...), custom_call_target="tpu_custom_call" | custom-call | flops 10737418240 | bytes 14680064 | tf_op jit(solution)/shard_map/pallas_call | solution.py:82
  121.8 0.0 copy-start.4
  121.8 0.0 copy-start.2
  121.8 3.7 %all-to-all-done.2 = f32[16,16,256]{2,1,0:T(8,128)S(1)} async-done(((f32[16,16,256]{2,1,0:T(8,128)}), f32[16,16,256]{2,1,0:T(8,128)S(1)}, u32[]{:S(2)}, u32[]{:S(2)}) %all-to-all-start.2) | async-done | bytes 262176 | tf_op jit(solution)/shard_map/all_to_all | solution.py:114
  125.5 4.6 %collective-permute-start.6 = (bf16[1024,256]{1,0:T(8,128)(2,1)}, bf16[1024,256]{1,0:T(8,128)(2,1)S(1)}, u32[]{:S(2)}, u32[]{:S(2)}) collective-permute-start(bf16[1024,256]{1,0:T(8,128)(2,1)} %get-tuple-element.28), channel_id=1, source_target_pairs={{0,64},{64,128},{128,192},{192,0},{1,65},{65,129},{129,193},{193,1... | collective-permute-start | bytes 1572872 | tf_op jit(solution)/shard_map/ppermute | solution.py:128
  130.1 0.0 collective-permute-start.7
  130.2 9.4 %all_to_all.27 = f32[16,16,256]{2,1,0:T(8,128)S(1)} all-to-all(f32[16,16,256]{2,1,0:T(8,128)S(1)} %broadcast_in_dim.36), channel_id=1, replica_groups=mesh['row_far'=4,'row_near'=4,'col_far'=4,'col_mid'=2,'col_near'=2] {'co..., dimensions={0} | all-to-all | bytes 524288 | tf_op jit(solution)/shard_map/all_to_all | solution.py:114
  139.6 0.2 collective-permute-done.6
  139.8 0.0 collective-permute-done.7
  139.8 1.1 add_convert_fusion.4
  140.9 1.1 collective-permute-start.8
  142.0 0.0 copy-done.4
  142.0 0.1 add_convert_fusion.2
  142.1 2.3 %collective-permute-start.9 = (bf16[512,256]{1,0:T(8,128)(2,1)S(1)}, bf16[512,256]{1,0:T(8,128)(2,1)S(1)}, u32[]{:S(2)}, u32[]{:S(2)}) collective-permute-start(bf16[512,256]{1,0:T(8,128)(2,1)S(1)} %add_convert_fusion.2), channel_id=1, source_target_pairs={{0,192},{64,0},{128,64},{192,128},{1,193},{65,1},{129,65},{193,129... | collective-permute-start | bytes 786440 | tf_op jit(solution)/shard_map/ppermute | solution.py:128
  144.4 6.6 %collective-permute-done.8 = bf16[512,256]{1,0:T(8,128)(2,1)S(1)} collective-permute-done((bf16[512,256]{1,0:T(8,128)(2,1)S(1)}, bf16[512,256]{1,0:T(8,128)(2,1)S(1)}, u32[]{:S(2)}, u32[]{:S(2)}) %collective-permute-start.8) | collective-permute-done | bytes 262176 | tf_op jit(solution)/shard_map/ppermute | solution.py:128
  150.9 0.0 collective-permute-done.9
  150.9 0.0 copy-done.2
  151.0 0.2 add_convert_fusion.3
  151.1 0.8 pad_maximum_fusion.1
  151.9 8.1 %all-to-all-start.4 = ((bf16[4,256,256]{2,1,0:T(8,128)(2,1)}), bf16[4,256,256]{2,1,0:T(8,128)(2,1)S(1)}, u32[]{:S(2)}, u32[]{:S(2)}) async-start(bf16[4,256,256]{2,1,0:T(8,128)(2,1)} %bitcast.10), calls=%async_computation.4 | async-start | bytes 1048576 | tf_op jit(solution)/shard_map/all_to_all | solution.py:114
  160.0 15.6 %all-to-all-done.4 = bf16[4,256,256]{2,1,0:T(8,128)(2,1)S(1)} async-done(((bf16[4,256,256]{2,1,0:T(8,128)(2,1)}), bf16[4,256,256]{2,1,0:T(8,128)(2,1)S(1)}, u32[]{:S(2)}, u32[]{:S(2)}) %all-to-all-start.4) | async-done | bytes 524320 | tf_op jit(solution)/shard_map/all_to_all | solution.py:114
  175.6 0.1 reduce_sum.55
  175.7 0.9 convolution_convert_fusion
  176.6 0.7 copy.12
  (13 shorter events, 0.1 us)
Async XLA Ops:
  0.6 81.9 %copy-start = (bf16[256,256]{1,0:T(8,128)(2,1)S(1)}, bf16[256,256]{1,0:T(8,128)(2,1)}, u32[]{:S(2)}) copy-start(bf16[256,256]{1,0:T(8,128)(2,1)} %param.8) | copy-start | bytes 393220
  21.1 22.8 %copy-start.3 = (bf16[1024,256]{1,0:T(8,128)(2,1)}, bf16[1024,256]{1,0:T(8,128)(2,1)S(1)}, u32[]{:S(2)}) copy-start(bf16[1024,256]{1,0:T(8,128)(2,1)S(1)} %all_gather.3) | copy-start | bytes 1572868
  21.1 11.5 %collective-permute-start.1 = (bf16[1024,256]{1,0:T(8,128)(2,1)S(1)}, bf16[1024,256]{1,0:T(8,128)(2,1)S(1)}, u32[]{:S(2)}, u32[]{:S(2)}) collective-permute-start(bf16[1024,256]{1,0:T(8,128)(2,1)S(1)} %all_gather.3), channel_id=1, source_target_pairs={{0,192},{64,0},{128,64},{192,128},{1,193},{65,1},{129,65},{193,129... | collective-permute-start | bytes 1572872 | tf_op jit(solution)/shard_map/ppermute | solution.py:128
  24.1 12.1 %collective-permute-start = (bf16[1024,256]{1,0:T(8,128)(2,1)S(1)}, bf16[1024,256]{1,0:T(8,128)(2,1)S(1)}, u32[]{:S(2)}, u32[]{:S(2)}) collective-permute-start(bf16[1024,256]{1,0:T(8,128)(2,1)S(1)} %all_gather.3), channel_id=1, source_target_pairs={{0,64},{64,128},{128,192},{192,0},{1,65},{65,129},{129,193},{193,1... | collective-permute-start | bytes 1572872 | tf_op jit(solution)/shard_map/ppermute | solution.py:128
  32.5 11.4 %copy-start.5 = (bf16[1024,256]{1,0:T(8,128)(2,1)}, bf16[1024,256]{1,0:T(8,128)(2,1)S(1)}, u32[]{:S(2)}) copy-start(bf16[1024,256]{1,0:T(8,128)(2,1)S(1)} %collective-permute-done.1) | copy-start | bytes 1572868
  32.5 7.6 %collective-permute-start.3 = (bf16[512,256]{1,0:T(8,128)(2,1)S(1)}, bf16[512,256]{1,0:T(8,128)(2,1)S(1)}, u32[]{:S(2)}, u32[]{:S(2)}) collective-permute-start(bf16[512,256]{1,0:T(8,128)(2,1)S(1)} %slice.41), channel_id=1, source_target_pairs={{0,192},{64,0},{128,64},{192,128},{1,193},{65,1},{129,65},{193,129... | collective-permute-start | bytes 786440 | tf_op jit(solution)/shard_map/ppermute | solution.py:128
  36.2 7.7 %copy-start.6 = (bf16[1024,256]{1,0:T(8,128)(2,1)}, bf16[1024,256]{1,0:T(8,128)(2,1)S(1)}, u32[]{:S(2)}) copy-start(bf16[1024,256]{1,0:T(8,128)(2,1)S(1)} %collective-permute-done) | copy-start | bytes 1572868
  36.2 7.7 %collective-permute-start.2 = (bf16[512,256]{1,0:T(8,128)(2,1)S(1)}, bf16[512,256]{1,0:T(8,128)(2,1)S(1)}, u32[]{:S(2)}, u32[]{:S(2)}) collective-permute-start(bf16[512,256]{1,0:T(8,128)(2,1)S(1)} %slice.40), channel_id=1, source_target_pairs={{0,64},{64,128},{128,192},{192,0},{1,65},{65,129},{129,193},{193,1... | collective-permute-start | bytes 786440 | tf_op jit(solution)/shard_map/ppermute | solution.py:128
  40.1 3.8 %copy-start.8 = (bf16[512,256]{1,0:T(8,128)(2,1)}, bf16[512,256]{1,0:T(8,128)(2,1)S(1)}, u32[]{:S(2)}) copy-start(bf16[512,256]{1,0:T(8,128)(2,1)S(1)} %collective-permute-done.3) | copy-start | bytes 786436
  43.9 0.7 copy-start.9
  54.0 3.0 %collective-permute-start.4 = (bf16[2048,256]{1,0:T(8,128)(2,1)}, bf16[2048,256]{1,0:T(8,128)(2,1)S(1)}, u32[]{:S(2)}, u32[]{:S(2)}) collective-permute-start(bf16[2048,256]{1,0:T(8,128)(2,1)} %get-tuple-element.20), channel_id=1, source_target_pairs={{0,1},{1,0},{2,3},{3,2},{4,5},{5,4},{6,7},{7,6},{8,9},{9,8},{10,11... | collective-permute-start | bytes 3145736 | tf_op jit(solution)/shard_map/ppermute | solution.py:128
  58.8 23.7 %copy-start.10 = (bf16[256,256]{1,0:T(8,128)(2,1)S(1)}, bf16[256,256]{1,0:T(8,128)(2,1)}, u32[]{:S(2)}) copy-start(bf16[256,256]{1,0:T(8,128)(2,1)} %param.13) | copy-start | bytes 393220
  103.4 8.6 %copy-start.1 = (bf16[8,288,256]{2,1,0:T(8,128)(2,1)}, bf16[8,288,256]{2,1,0:T(8,128)(2,1)S(1)}, u32[]{:S(2)}) copy-start(bf16[8,288,256]{2,1,0:T(8,128)(2,1)S(1)} %all_to_all.26.refs_0_) | copy-start | bytes 3538948
  103.4 2.8 %collective-permute-start.5 = (bf16[8,288,256]{2,1,0:T(8,128)(2,1)S(1)}, bf16[8,288,256]{2,1,0:T(8,128)(2,1)S(1)}, u32[]{:S(2)}, u32[]{:S(2)}) collective-permute-start(bf16[8,288,256]{2,1,0:T(8,128)(2,1)S(1)} %all_to_all.26.refs_0_), channel_id=1, source_target_pairs={{0,1},{1,0},{2,3},{3,2},{4,5},{5,4},{6,7},{7,6},{8,9},{9,8},{10,11... | collective-permute-start | bytes 3538952 | tf_op jit(solution)/shard_map/ppermute | solution.py:128
  106.2 5.8 %copy-start.7 = (bf16[8,288,256]{2,1,0:T(8,128)(2,1)}, bf16[8,288,256]{2,1,0:T(8,128)(2,1)S(1)}, u32[]{:S(2)}) copy-start(bf16[8,288,256]{2,1,0:T(8,128)(2,1)S(1)} %collective-permute-done.5.refs_1_) | copy-start | bytes 3538948
  107.2 18.4 %all-to-all-start.2 = ((f32[16,16,256]{2,1,0:T(8,128)}), f32[16,16,256]{2,1,0:T(8,128)S(1)}, u32[]{:S(2)}, u32[]{:S(2)}) async-start(f32[16,16,256]{2,1,0:T(8,128)} %broadcast_in_dim.35), calls=%async_computation.2 | async-start | bytes 524288 | tf_op jit(solution)/shard_map/all_to_all | solution.py:114
  121.8 20.2 %copy-start.4 = (f32[512,256]{1,0:T(8,128)S(1)}, f32[512,256]{1,0:T(8,128)}, u32[]{:S(2)}) copy-start(f32[512,256]{1,0:T(8,128)} %get-tuple-element.33) | copy-start | bytes 1572868
  121.8 29.2 %copy-start.2 = (f32[1024,256]{1,0:T(8,128)S(1)}, f32[1024,256]{1,0:T(8,128)}, u32[]{:S(2)}) copy-start(f32[1024,256]{1,0:T(8,128)} %get-tuple-element.23) | copy-start | bytes 3145732
  125.5 14.3 %collective-permute-start.6 = (bf16[1024,256]{1,0:T(8,128)(2,1)}, bf16[1024,256]{1,0:T(8,128)(2,1)S(1)}, u32[]{:S(2)}, u32[]{:S(2)}) collective-permute-start(bf16[1024,256]{1,0:T(8,128)(2,1)} %get-tuple-element.28), channel_id=1, source_target_pairs={{0,64},{64,128},{128,192},{192,0},{1,65},{65,129},{129,193},{193,1... | collective-permute-start | bytes 1572872 | tf_op jit(solution)/shard_map/ppermute | solution.py:128
  130.1 9.7 %collective-permute-start.7 = (bf16[1024,256]{1,0:T(8,128)(2,1)}, bf16[1024,256]{1,0:T(8,128)(2,1)S(1)}, u32[]{:S(2)}, u32[]{:S(2)}) collective-permute-start(bf16[1024,256]{1,0:T(8,128)(2,1)} %get-tuple-element.29), channel_id=1, source_target_pairs={{0,192},{64,0},{128,64},{192,128},{1,193},{65,1},{129,65},{193,129... | collective-permute-start | bytes 1572872 | tf_op jit(solution)/shard_map/ppermute | solution.py:128
  140.9 10.0 %collective-permute-start.8 = (bf16[512,256]{1,0:T(8,128)(2,1)S(1)}, bf16[512,256]{1,0:T(8,128)(2,1)S(1)}, u32[]{:S(2)}, u32[]{:S(2)}) collective-permute-start(bf16[512,256]{1,0:T(8,128)(2,1)S(1)} %add_convert_fusion.4), channel_id=1, source_target_pairs={{0,64},{64,128},{128,192},{192,0},{1,65},{65,129},{129,193},{193,1... | collective-permute-start | bytes 786440 | tf_op jit(solution)/shard_map/ppermute | solution.py:128
  142.1 8.9 %collective-permute-start.9 = (bf16[512,256]{1,0:T(8,128)(2,1)S(1)}, bf16[512,256]{1,0:T(8,128)(2,1)S(1)}, u32[]{:S(2)}, u32[]{:S(2)}) collective-permute-start(bf16[512,256]{1,0:T(8,128)(2,1)S(1)} %add_convert_fusion.2), channel_id=1, source_target_pairs={{0,192},{64,0},{128,64},{192,128},{1,193},{65,1},{129,65},{193,129... | collective-permute-start | bytes 786440 | tf_op jit(solution)/shard_map/ppermute | solution.py:128
  151.9 23.7 %all-to-all-start.4 = ((bf16[4,256,256]{2,1,0:T(8,128)(2,1)}), bf16[4,256,256]{2,1,0:T(8,128)(2,1)S(1)}, u32[]{:S(2)}, u32[]{:S(2)}) async-start(bf16[4,256,256]{2,1,0:T(8,128)(2,1)} %bitcast.10), calls=%async_computation.4 | async-start | bytes 1048576 | tf_op jit(solution)/shard_map/all_to_all | solution.py:114

commit v3 on v2

--- a/solution.py
+++ b/solution.py
@@ -12,61 +12,73 @@
     return jax.nn.gelu(value, approximate=True)
 
 
-def tile_kernel(count_ref, put_ref, take_ref, tiles_ref, *refs, pieces, outs, unroll, transpose):
-    piece_refs, out_refs = refs[: len(pieces)], refs[len(pieces) : len(pieces) + outs]
-    source_ref, sum_ref, arrived = refs[len(pieces) + outs :]
-    step = pl.program_id(0)
-    group, size, _ = tiles_ref.shape
+def tile_kernel(count_ref, put_ref, take_ref, tiles_hbm, *refs, pieces, outs, group, transpose):
+    piece_refs, out_refs = refs[: len(pieces)], refs[len(pieces) : len(pieces) + len(outs)]
+    tiles_ref, source_ref, sum_ref, *rounded, tiles_in, source_in, out_sent = refs[len(pieces) + len(outs) :]
+    size = tiles_ref.shape[-1]
     spare = sum_ref.shape[0] // size - 1
     live = count_ref[0]
-    first = step * group
     contract = (((0,), (0,)), ((), ())) if transpose else (((1,), (0,)), ((), ()))
 
-    @pl.when(step == 0)
-    def _():
-        copies, at = [], 0
-        for piece, (blocks, rows) in zip(piece_refs, pieces):
-            for block in range(blocks):
-                copies.append(
-                    pltpu.make_async_copy(
-                        piece.at[block, pl.ds(0, rows), :],
-                        source_ref.at[pl.ds(at, rows), :],
-                        arrived.at[len(copies)],
-                    )
+    def tiles_copy(index):
+        some = pl.ds(pl.multiple_of(index * group, group), group)
+        return pltpu.make_async_copy(tiles_hbm.at[some], tiles_ref.at[some], tiles_in.at[index])
+
+    copies, at = [], 0
+    for piece, (blocks, rows) in zip(piece_refs, pieces):
+        for block in range(blocks):
+            copies.append(
+                pltpu.make_async_copy(
+                    piece.at[block, pl.ds(0, rows), :],
+                    source_ref.at[pl.ds(at, rows), :],
+                    source_in.at[len(copies)],
                 )
-                at += rows
-        for copy in copies:
-            copy.start()
-        sum_ref[...] = jnp.zeros_like(sum_ref)
-        for copy in copies:
-            copy.wait()
+            )
+            at += rows
+    for copy in copies:
+        copy.start()
+    batches = (live + group - 1) // group
+
+    def begin(index, carry):
+        tiles_copy(index).start()
+        return carry
+
+    lax.fori_loop(0, batches, begin, 0)
+    sum_ref[...] = jnp.zeros_like(sum_ref)
+    for copy in copies:
+        copy.wait()
 
     def batch(index, carry):
+        tiles_copy(index).wait()
         rows, products = [], []
-        for lane in range(unroll):
-            place = index * unroll + lane
-            slot = first + place
+        for lane in range(group):
+            slot = index * group + lane
             used = slot < live
             put = jnp.where(used, put_ref[slot], spare)
             take = jnp.where(used, take_ref[slot], 0)
             picked = source_ref[pl.ds(pl.multiple_of(take * size, size), size), :]
             rows.append(pl.multiple_of(put * size, size))
             products.append(
-                lax.dot_general(tiles_ref[place], picked, contract, preferred_element_type=jnp.float32)
+                lax.dot_general(tiles_ref[slot], picked, contract, preferred_element_type=jnp.float32)
             )
         for row, product in zip(rows, products):
             sum_ref[pl.ds(row, size), :] += product
         return carry
 
-    todo = jnp.clip(live - first, 0, group)
-    lax.fori_loop(0, (todo + unroll - 1) // unroll, batch, 0)
-
-    @pl.when(step == pl.num_programs(0) - 1)
-    def _():
-        at = 0
-        for out in out_refs:
-            out[...] = sum_ref[pl.ds(at, out.shape[0]), :].astype(out.dtype)
-            at += out.shape[0]
+    lax.fori_loop(0, batches, batch, 0)
+
+    writes, at = [], 0
+    for out in out_refs:
+        part = sum_ref.at[pl.ds(at, out.shape[0]), :]
+        at += out.shape[0]
+        if out.dtype != sum_ref.dtype:
+            narrow = rounded.pop(0)
+            narrow[...] = part[...].astype(out.dtype)
+            part = narrow
+        writes.append(pltpu.make_async_copy(part, out, out_sent.at[len(writes)]))
+        writes[-1].start()
+    for write in writes:
+        write.wait()
 
 
 def tile_products(live_count, put_ids, take_ids, block_tiles, sources, rows_used, outs, transpose):
@@ -77,30 +89,23 @@
     source_rows = sum(blocks * rows for blocks, rows in pieces)
     sum_rows = sum(rows for rows, _ in outs)
     group = math.gcd(slots, 32)
-    unroll = math.gcd(group, 16)
-    whole = lambda i, *_: (0, 0)
+    anywhere = pl.BlockSpec(memory_space=pl.ANY)
     return pl.pallas_call(
-        functools.partial(
-            tile_kernel, pieces=pieces, outs=len(outs), unroll=unroll, transpose=transpose
-        ),
+        functools.partial(tile_kernel, pieces=pieces, outs=outs, group=group, transpose=transpose),
         out_shape=[jax.ShapeDtypeStruct((rows, width), kind) for rows, kind in outs],
-        grid_spec=pltpu.PrefetchScalarGridSpec(
-            num_scalar_prefetch=3,
-            grid=(slots // group,),
-            in_specs=[
-                pl.BlockSpec(
-                    (group, size, size),
-                    lambda i, count, put, take: (jnp.minimum(i, jnp.maximum(count[0] - 1, 0) // group), 0, 0),
-                )
-            ]
-            + [pl.BlockSpec(memory_space=pl.ANY)] * len(pieces),
-            out_specs=[pl.BlockSpec((rows, width), whole) for rows, _ in outs],
-            scratch_shapes=[
-                pltpu.VMEM((source_rows, width), jnp.bfloat16),
-                pltpu.VMEM((sum_rows + size, width), jnp.float32),
-                pltpu.SemaphoreType.DMA((sum(blocks for blocks, _ in pieces),)),
-            ],
-        ),
+        in_specs=[pl.BlockSpec(memory_space=pltpu.SMEM)] * 3 + [anywhere] * (1 + len(sources)),
+        out_specs=[anywhere] * len(outs),
+        scratch_shapes=[
+            pltpu.VMEM((slots, size, size), jnp.bfloat16),
+            pltpu.VMEM((source_rows, width), jnp.bfloat16),
+            pltpu.VMEM((sum_rows + size, width), jnp.float32),
+        ]
+        + [pltpu.VMEM((rows, width), kind) for rows, kind in outs if kind != jnp.float32]
+        + [
+            pltpu.SemaphoreType.DMA((slots // group,)),
+            pltpu.SemaphoreType.DMA((sum(blocks for blocks, _ in pieces),)),
+            pltpu.SemaphoreType.DMA((len(outs),)),
+        ],
         compiler_params=pltpu.CompilerParams(vmem_limit_bytes=56 << 20),
         cost_estimate=pl.CostEstimate(
             flops=8 * slots * size * size * width,
@@ -117,6 +122,10 @@
 def spread(block, axes):
     devices = lax.axis_size(axes)
     return exchange(lax.optimization_barrier(jnp.broadcast_to(block[None], (devices,) + block.shape)), axes)
+
+
+def add(*parts):
+    return sum(part.astype(jnp.float32) for part in parts).astype(jnp.bfloat16)
 
 
 def total(parts):
@@ -176,9 +185,9 @@
     low, high = shift(left[:half_rows], "row_far", 1), shift(right[half_rows:], "row_far", -1)
     keep, send = tile_products(
         live_count, row_place, col_take, block_tiles, [own, left, right, low, high], None,
-        [(mid_rows, jnp.float32), (mid_rows, jnp.bfloat16)], False,
-    )
-    paired = (keep + shift(send, "col_near", 1).astype(jnp.float32)).astype(jnp.bfloat16)
+        [(mid_rows, jnp.bfloat16)] * 2, False,
+    )
+    paired = add(keep, shift(send, "col_near", 1))
     parts = exchange(paired.reshape(mid, seg_rows, feat_width), ("col_far", "col_mid"))
     aggregated = total(parts).astype(jnp.bfloat16)
 
@@ -208,13 +217,7 @@
 
     own, right_one, left_one, right_two, left_two = tile_products(
         live_count, col_put, row_place, block_tiles, [mine, theirs], seg_rows,
-        [
-            (far_rows, jnp.float32),
-            (far_rows, jnp.bfloat16),
-            (far_rows, jnp.bfloat16),
-            (half_rows, jnp.float32),
-            (half_rows, jnp.float32),
-        ],
+        [(far_rows, jnp.bfloat16)] * 3 + [(half_rows, jnp.bfloat16)] * 2,
         True,
     )
     right_one, left_one, weight_slices = lax.optimization_barrier((right_one, left_one, weight_slices))
@@ -222,12 +225,11 @@
     weight_slice = total(weight_slices) * (1.0 / math.sqrt(node_total))
     weight_grad = spread(weight_slice, col).reshape(feat_width, feat_width)
     from_left, from_right, weight_grad = lax.optimization_barrier((from_left, from_right, weight_grad))
-    right_two = (right_two + from_left[:half_rows].astype(jnp.float32)).astype(jnp.bfloat16)
-    left_two = (left_two + from_right[half_rows:].astype(jnp.float32)).astype(jnp.bfloat16)
+    right_two, left_two = add(right_two, from_left[:half_rows]), add(left_two, from_right[half_rows:])
     low, high = shift(right_two, "row_far", 1), shift(left_two, "row_far", -1)
-    low = own[:half_rows] + low.astype(jnp.float32) + from_right[:half_rows].astype(jnp.float32)
-    high = own[half_rows:] + high.astype(jnp.float32) + from_left[half_rows:].astype(jnp.float32)
-    mixed = jnp.concatenate([low, high], axis=0).astype(jnp.bfloat16)
+    low = add(own[:half_rows], low, from_right[:half_rows])
+    high = add(own[half_rows:], high, from_left[half_rows:])
+    mixed = jnp.concatenate([low, high], axis=0)
     parts = exchange(mixed.reshape(near, seg_rows, feat_width), "row_near")
     back_sum = total(parts).astype(jnp.bfloat16)
 

time: 179 us -> 170 us (0.950)
  Pallas kernels: 19.1 us -> 11.4 us
  starting transfers between devices: 27.8 us -> 20.8 us
  waiting for transfers between devices: 45.1 us -> 51.4 us
  other arithmetic: 6.47 us -> 3.75 us
    pallas_call x2, Pallas kernels: 19.1 us -> 11.4 us  [tile_products(): pl.pallas_call(functools.partial(tile_kernel, pieces=pieces, outs=outs, g...]
    all_to_all x2, starting transfers between devices: 12.9 us -> 7.64 us  [exchange(): return lax.all_to_all(chunks, axes, 0, 0)]
    all_to_all x2, waiting for transfers between devices: 19.3 us -> 22.6 us  [exchange(): return lax.all_to_all(chunks, axes, 0, 0)]
    ppermute x10, waiting for transfers between devices: 25.8 us -> 28.9 us  [shift(): lax.ppermute(block, axis, [(k, (k + by) % devices) for k in range(devices)])]
  transfers between devices with their start and end apart: 12 -> 12, of which waited for: 9 -> 10; matrix products, arithmetic and copies ran while one was open for 1% -> 0% of each run, Pallas kernels for 5% -> 3%
where the time goes in v3:
time: 170 us; the launch traced here: 168 us
  blocking collectives  74.3 us (44%)
  waiting for transfers between devices  51.4 us (30%)
  starting transfers between devices  20.8 us (12%)
  Pallas kernels  11.4 us (7%)
  other arithmetic  3.75 us (2%)
  local copies, waits for them, and re-layouts  2.42 us (1%)
  matrix products  2.12 us (1%)
    all_to_all x3, blocking collectives, exchange(): return lax.all_to_all(chunks, axes, 0, 0)  53.9 us
    ppermute x10, waiting for transfers between devices, shift(): lax.ppermute(block, axis, [(k, (k + by) % devices) for k in range(devices)])  28.9 us
    all_to_all x2, waiting for transfers between devices, exchange(): return lax.all_to_all(chunks, axes, 0, 0)  22.6 us
    all_gather x1, blocking collectives, on_device(): own = lax.all_gather(features, 'row_near', axis=0, tiled=True)  20.4 us
    ppermute x10, starting transfers between devices, shift(): lax.ppermute(block, axis, [(k, (k + by) % devices) for k in range(devices)])  13.2 us
    pallas_call x2, Pallas kernels, tile_products(): pl.pallas_call(functools.partial(tile_kernel, pieces=pieces, outs=outs, g...  11.4 us
    all_to_all x2, starting transfers between devices, exchange(): return lax.all_to_all(chunks, axes, 0, 0)  7.64 us
  transfers between devices with their start and end apart: 12, of which 10 were waited for; matrix products, arithmetic and copies ran while one was open for 0% of the time, Pallas kernels for 3%

profile of v3, /device:TPU:2, one launch (start us, length us, event | category | flops | bytes accessed | tf_op | source)
XLA Modules:
  0.0 167.9 jit_solution(12206016721989837160)
XLA Ops:
  0.6 0.0 copy-start
  0.6 0.0 copy-start.9
  0.7 0.0 copy-start.10
  0.7 20.4 %all_gather.3 = bf16[1024,256]{1,0:T(8,128)(2,1)S(1)} all-gather(bf16[256,256]{1,0:T(8,128)(2,1)} %param.7), channel_id=1, replica_groups=mesh['row_far'=4,'row_near'=4,'col_far'=4,'col_mid'=2,'col_near'=2] {'ro..., dimensions={0}, use_global_device_ids=true | all-gather | bytes 655360 | tf_op jit(solution)/shard_map/all_gather | solution.py:183
  21.1 3.0 %collective-permute-start.1 = (bf16[1024,256]{1,0:T(8,128)(2,1)S(1)}, bf16[1024,256]{1,0:T(8,128)(2,1)S(1)}, u32[]{:S(2)}, u32[]{:S(2)}) collective-permute-start(bf16[1024,256]{1,0:T(8,128)(2,1)S(1)} %all_gather.3), channel_id=1, source_target_pairs={{0,192},{64,0},{128,64},{192,128},{1,193},{65,1},{129,65},{193,129... | collective-permute-start | bytes 1572872 | tf_op jit(solution)/shard_map/ppermute | solution.py:137
  24.1 0.0 collective-permute-start
  24.1 8.4 %collective-permute-done.1 = bf16[1024,256]{1,0:T(8,128)(2,1)S(1)} collective-permute-done((bf16[1024,256]{1,0:T(8,128)(2,1)S(1)}, bf16[1024,256]{1,0:T(8,128)(2,1)S(1)}, u32[]{:S(2)}, u32[]{:S(2)}) %collective-permute-start.1) | collective-permute-done | bytes 524320 | tf_op jit(solution)/shard_map/ppermute | solution.py:137
  32.6 3.7 %collective-permute-start.3 = (bf16[512,256]{1,0:T(8,128)(2,1)S(1)}, bf16[512,256]{1,0:T(8,128)(2,1)S(1)}, u32[]{:S(2)}, u32[]{:S(2)}) collective-permute-start(bf16[512,256]{1,0:T(8,128)(2,1)S(1)} %slice.41), channel_id=1, source_target_pairs={{0,192},{64,0},{128,64},{192,128},{1,193},{65,1},{129,65},{193,129... | collective-permute-start | bytes 786440 | tf_op jit(solution)/shard_map/ppermute | solution.py:137
  36.2 0.0 collective-permute-done
  36.2 0.1 collective-permute-start.2
  37.0 0.0 copy-done.9
  37.1 0.0 copy-done.10
  37.1 0.6 select_add_fusion
  37.7 2.4 %collective-permute-done.3 = bf16[512,256]{1,0:T(8,128)(2,1)S(1)} collective-permute-done((bf16[512,256]{1,0:T(8,128)(2,1)S(1)}, bf16[512,256]{1,0:T(8,128)(2,1)S(1)}, u32[]{:S(2)}, u32[]{:S(2)}) %collective-permute-start.3) | collective-permute-done | bytes 262176 | tf_op jit(solution)/shard_map/ppermute | solution.py:137
  40.1 3.8 %collective-permute-done.2 = bf16[512,256]{1,0:T(8,128)(2,1)S(1)} collective-permute-done((bf16[512,256]{1,0:T(8,128)(2,1)S(1)}, bf16[512,256]{1,0:T(8,128)(2,1)S(1)}, u32[]{:S(2)}, u32[]{:S(2)}) %collective-permute-start.2) | collective-permute-done | bytes 262176 | tf_op jit(solution)/shard_map/ppermute | solution.py:137
  43.9 0.0 copy-done.2
  43.9 0.0 copy-done.6
  43.9 0.0 copy-done.7
  43.9 0.0 copy-done.11
  43.9 0.7 copy-done.12
  44.6 5.6 %shard_map.94 = (bf16[2048,256]{1,0:T(8,128)(2,1)}, bf16[2048,256]{1,0:T(8,128)(2,1)}) custom-call(s32[1]{0:T(128)} %bitcast.17.count_ref, s32[320]{0:T(512)} %get-tuple-element.41.put_ref.take_ref, s32[320]{0:T(512)} %get-tuple-element.40.take_ref, bf16[320,128,128]{2,1,0:T(8,128)(2,1)} %bitcast.25, bf16[1,1024,256]{2,1,0:T(8,128)(2,1)} %bitcast.22, ...), custom_call_target="tpu_custom_call" | custom-call | flops 10737418240 | bytes 14680064 | tf_op jit(solution)/shard_map/pallas_call | solution.py:93
  50.2 0.1 collective-permute-start.4
  50.3 2.9 %collective-permute-done.4 = bf16[2048,256]{1,0:T(8,128)(2,1)S(1)} collective-permute-done((bf16[2048,256]{1,0:T(8,128)(2,1)}, bf16[2048,256]{1,0:T(8,128)(2,1)S(1)}, u32[]{:S(2)}, u32[]{:S(2)}) %collective-permute-start.4) | collective-permute-done | bytes 1048608 | tf_op jit(solution)/shard_map/ppermute | solution.py:137
  53.2 1.5 add_convert_fusion
  54.7 0.0 copy-start.13
  54.7 24.7 %all_to_all.25 = bf16[8,256,256]{2,1,0:T(8,128)(2,1)S(1)} all-to-all(bf16[8,256,256]{2,1,0:T(8,128)(2,1)S(1)} %bitcast.19), channel_id=1, replica_groups=mesh['row_far'=4,'row_near'=4,'col_far'=4,'col_mid'=2,'col_near'=2] {'co..., dimensions={0} | all-to-all | bytes 2097152 | tf_op jit(solution)/shard_map/all_to_all | solution.py:119
  79.4 0.1 reduce_sum.51
  79.5 0.0 copy-done
  79.6 0.0 copy-done.13
  79.6 1.0 fusion.2
  80.6 0.2 convolution_convert_fusion.1
  80.8 0.1 broadcast_in_dim.34
  80.9 0.1 pad_maximum_fusion
  81.0 19.4 %all_to_all.26.refs_0_ = bf16[8,288,256]{2,1,0:T(8,128)(2,1)S(1)} all-to-all(bf16[8,288,256]{2,1,0:T(8,128)(2,1)S(1)} %pad_maximum_fusion), channel_id=1, replica_groups=mesh['row_far'=4,'row_near'=4,'col_far'=4,'col_mid'=2,'col_near'=2] {'co..., dimensions={0} | all-to-all | bytes 2359296 | tf_op jit(solution)/shard_map/all_to_all | solution.py:119
  100.4 0.0 collective-permute-start.5
  100.4 2.8 %collective-permute-done.5.refs_1_ = bf16[8,288,256]{2,1,0:T(8,128)(2,1)S(1)} collective-permute-done((bf16[8,288,256]{2,1,0:T(8,128)(2,1)S(1)}, bf16[8,288,256]{2,1,0:T(8,128)(2,1)S(1)}, u32[]{:S(2)}, u32[]{:S(2)}) %collective-permute-start.5) | collective-permute-done | bytes 1179680 | tf_op jit(solution)/shard_map/ppermute | solution.py:137
  103.3 0.9 broadcast_in_dim.35
  104.1 3.7 %all-to-all-start.2 = ((f32[16,16,256]{2,1,0:T(8,128)}), f32[16,16,256]{2,1,0:T(8,128)S(1)}, u32[]{:S(2)}, u32[]{:S(2)}) async-start(f32[16,16,256]{2,1,0:T(8,128)} %broadcast_in_dim.35), calls=%async_computation.2 | async-start | bytes 524288 | tf_op jit(solution)/shard_map/all_to_all | solution.py:119
  107.9 0.0 copy-done.1
  107.9 0.0 copy-done.8
  107.9 5.8 %shard_map.95 = (bf16[1024,256]{1,0:T(8,128)(2,1)}, bf16[1024,256]{1,0:T(8,128)(2,1)}, bf16[1024,256]{1,0:T(8,128)(2,1)}, bf16[512,256]{1,0:T(8,128)(2,1)}, bf16[512,256]{1,0:T(8,128)(2,1)}) custom-call(s32[1]{0:T(128)} %bitcast.18.count_ref, s32[320]{0:T(512)} %get-tuple-element.39.put_ref, s32[320]{0:T(512)} %get-tuple-element.41.put_ref.take_ref, ...), custom_call_target="tpu_custom_call" | custom-call | flops 10737418240 | bytes 14680064 | tf_op jit(solution)/shard_map/pallas_call | solution.py:93
  113.7 0.0 copy-start.4
  113.7 7.9 %all-to-all-done.2 = f32[16,16,256]{2,1,0:T(8,128)S(1)} async-done(((f32[16,16,256]{2,1,0:T(8,128)}), f32[16,16,256]{2,1,0:T(8,128)S(1)}, u32[]{:S(2)}, u32[]{:S(2)}) %all-to-all-start.2) | async-done | bytes 262176 | tf_op jit(solution)/shard_map/all_to_all | solution.py:119
  121.6 0.0 collective-permute-start.6
  121.6 3.2 %collective-permute-start.7 = (bf16[1024,256]{1,0:T(8,128)(2,1)}, bf16[1024,256]{1,0:T(8,128)(2,1)S(1)}, u32[]{:S(2)}, u32[]{:S(2)}) collective-permute-start(bf16[1024,256]{1,0:T(8,128)(2,1)} %get-tuple-element.29), channel_id=1, source_target_pairs={{0,192},{64,0},{128,64},{192,128},{1,193},{65,1},{129,65},{193,129... | collective-permute-start | bytes 1572872 | tf_op jit(solution)/shard_map/ppermute | solution.py:137
  124.9 9.9 %all_to_all.27 = f32[16,16,256]{2,1,0:T(8,128)S(1)} all-to-all(f32[16,16,256]{2,1,0:T(8,128)S(1)} %broadcast_in_dim.36), channel_id=1, replica_groups=mesh['row_far'=4,'row_near'=4,'col_far'=4,'col_mid'=2,'col_near'=2] {'co..., dimensions={0} | all-to-all | bytes 524288 | tf_op jit(solution)/shard_map/all_to_all | solution.py:119
  134.7 1.0 collective-permute-done.6
  135.7 0.0 collective-permute-done.7
  135.7 0.0 copy-done.5
  135.7 0.1 add_convert_fusion.2
  135.8 3.0 %collective-permute-start.9 = (bf16[512,256]{1,0:T(8,128)(2,1)S(1)}, bf16[512,256]{1,0:T(8,128)(2,1)S(1)}, u32[]{:S(2)}, u32[]{:S(2)}) collective-permute-start(bf16[512,256]{1,0:T(8,128)(2,1)S(1)} %add_convert_fusion.2), channel_id=1, source_target_pairs={{0,192},{64,0},{128,64},{192,128},{1,193},{65,1},{129,65},{193,129... | collective-permute-start | bytes 786440 | tf_op jit(solution)/shard_map/ppermute | solution.py:137
  138.8 0.0 copy-done.4
  138.8 0.1 add_convert_fusion.4
  138.9 0.1 collective-permute-start.8
  139.0 4.9 %collective-permute-done.9 = bf16[512,256]{1,0:T(8,128)(2,1)S(1)} collective-permute-done((bf16[512,256]{1,0:T(8,128)(2,1)S(1)}, bf16[512,256]{1,0:T(8,128)(2,1)S(1)}, u32[]{:S(2)}, u32[]{:S(2)}) %collective-permute-start.9) | collective-permute-done | bytes 262176 | tf_op jit(solution)/shard_map/ppermute | solution.py:137
  143.9 2.7 %collective-permute-done.8 = bf16[512,256]{1,0:T(8,128)(2,1)S(1)} collective-permute-done((bf16[512,256]{1,0:T(8,128)(2,1)S(1)}, bf16[512,256]{1,0:T(8,128)(2,1)S(1)}, u32[]{:S(2)}, u32[]{:S(2)}) %collective-permute-start.8) | collective-permute-done | bytes 262176 | tf_op jit(solution)/shard_map/ppermute | solution.py:137
  146.5 0.0 copy-done.3
  146.5 0.2 add_convert_fusion.3
  146.7 0.8 pad_maximum_fusion.1
  147.6 3.9 %all-to-all-start.4 = ((bf16[4,256,256]{2,1,0:T(8,128)(2,1)}), bf16[4,256,256]{2,1,0:T(8,128)(2,1)S(1)}, u32[]{:S(2)}, u32[]{:S(2)}) async-start(bf16[4,256,256]{2,1,0:T(8,128)(2,1)} %bitcast.10), calls=%async_computation.4 | async-start | bytes 1048576 | tf_op jit(solution)/shard_map/all_to_all | solution.py:119
  151.5 14.7 %all-to-all-done.4 = bf16[4,256,256]{2,1,0:T(8,128)(2,1)S(1)} async-done(((bf16[4,256,256]{2,1,0:T(8,128)(2,1)}), bf16[4,256,256]{2,1,0:T(8,128)(2,1)S(1)}, u32[]{:S(2)}, u32[]{:S(2)}) %all-to-all-start.4) | async-done | bytes 524320 | tf_op jit(solution)/shard_map/all_to_all | solution.py:119
  166.2 0.1 reduce_sum.55
  166.3 0.9 convolution_convert_fusion
  167.2 0.7 copy.12
  (19 shorter events, 0.2 us)
Async XLA Ops:
  0.6 78.9 %copy-start = (bf16[256,256]{1,0:T(8,128)(2,1)S(1)}, bf16[256,256]{1,0:T(8,128)(2,1)}, u32[]{:S(2)}) copy-start(bf16[256,256]{1,0:T(8,128)(2,1)} %param.8) | copy-start | bytes 393220
  0.6 36.4 %copy-start.9 = (s32[1,1,320]{2,1,0:T(1,128)S(1)}, s32[1,1,320]{2,1,0:T(1,128)}, u32[]{:S(2)}) copy-start(s32[1,1,320]{2,1,0:T(1,128)} %param.9) | copy-start | bytes 3844
  0.7 36.4 %copy-start.10 = (s32[1,1,320]{2,1,0:T(1,128)S(1)}, s32[1,1,320]{2,1,0:T(1,128)}, u32[]{:S(2)}) copy-start(s32[1,1,320]{2,1,0:T(1,128)} %param.10) | copy-start | bytes 3844
  21.1 22.8 %copy-start.2 = (bf16[1024,256]{1,0:T(8,128)(2,1)}, bf16[1024,256]{1,0:T(8,128)(2,1)S(1)}, u32[]{:S(2)}) copy-start(bf16[1024,256]{1,0:T(8,128)(2,1)S(1)} %all_gather.3) | copy-start | bytes 1572868
  21.1 11.5 %collective-permute-start.1 = (bf16[1024,256]{1,0:T(8,128)(2,1)S(1)}, bf16[1024,256]{1,0:T(8,128)(2,1)S(1)}, u32[]{:S(2)}, u32[]{:S(2)}) collective-permute-start(bf16[1024,256]{1,0:T(8,128)(2,1)S(1)} %all_gather.3), channel_id=1, source_target_pairs={{0,192},{64,0},{128,64},{192,128},{1,193},{65,1},{129,65},{193,129... | collective-permute-start | bytes 1572872 | tf_op jit(solution)/shard_map/ppermute | solution.py:137
  24.1 12.1 %collective-permute-start = (bf16[1024,256]{1,0:T(8,128)(2,1)S(1)}, bf16[1024,256]{1,0:T(8,128)(2,1)S(1)}, u32[]{:S(2)}, u32[]{:S(2)}) collective-permute-start(bf16[1024,256]{1,0:T(8,128)(2,1)S(1)} %all_gather.3), channel_id=1, source_target_pairs={{0,64},{64,128},{128,192},{192,0},{1,65},{65,129},{129,193},{193,1... | collective-permute-start | bytes 1572872 | tf_op jit(solution)/shard_map/ppermute | solution.py:137
  32.5 11.4 %copy-start.6 = (bf16[1024,256]{1,0:T(8,128)(2,1)}, bf16[1024,256]{1,0:T(8,128)(2,1)S(1)}, u32[]{:S(2)}) copy-start(bf16[1024,256]{1,0:T(8,128)(2,1)S(1)} %collective-permute-done.1) | copy-start | bytes 1572868
  32.6 7.6 %collective-permute-start.3 = (bf16[512,256]{1,0:T(8,128)(2,1)S(1)}, bf16[512,256]{1,0:T(8,128)(2,1)S(1)}, u32[]{:S(2)}, u32[]{:S(2)}) collective-permute-start(bf16[512,256]{1,0:T(8,128)(2,1)S(1)} %slice.41), channel_id=1, source_target_pairs={{0,192},{64,0},{128,64},{192,128},{1,193},{65,1},{129,65},{193,129... | collective-permute-start | bytes 786440 | tf_op jit(solution)/shard_map/ppermute | solution.py:137
  36.2 7.7 %copy-start.7 = (bf16[1024,256]{1,0:T(8,128)(2,1)}, bf16[1024,256]{1,0:T(8,128)(2,1)S(1)}, u32[]{:S(2)}) copy-start(bf16[1024,256]{1,0:T(8,128)(2,1)S(1)} %collective-permute-done) | copy-start | bytes 1572868
  36.2 7.7 %collective-permute-start.2 = (bf16[512,256]{1,0:T(8,128)(2,1)S(1)}, bf16[512,256]{1,0:T(8,128)(2,1)S(1)}, u32[]{:S(2)}, u32[]{:S(2)}) collective-permute-start(bf16[512,256]{1,0:T(8,128)(2,1)S(1)} %slice.40), channel_id=1, source_target_pairs={{0,64},{64,128},{128,192},{192,0},{1,65},{65,129},{129,193},{193,1... | collective-permute-start | bytes 786440 | tf_op jit(solution)/shard_map/ppermute | solution.py:137
  40.1 3.8 %copy-start.11 = (bf16[512,256]{1,0:T(8,128)(2,1)}, bf16[512,256]{1,0:T(8,128)(2,1)S(1)}, u32[]{:S(2)}) copy-start(bf16[512,256]{1,0:T(8,128)(2,1)S(1)} %collective-permute-done.3) | copy-start | bytes 786436
  43.9 0.7 copy-start.12
  50.2 3.0 %collective-permute-start.4 = (bf16[2048,256]{1,0:T(8,128)(2,1)}, bf16[2048,256]{1,0:T(8,128)(2,1)S(1)}, u32[]{:S(2)}, u32[]{:S(2)}) collective-permute-start(bf16[2048,256]{1,0:T(8,128)(2,1)} %get-tuple-element.20), channel_id=1, source_target_pairs={{0,1},{1,0},{2,3},{3,2},{4,5},{5,4},{6,7},{7,6},{8,9},{9,8},{10,11... | collective-permute-start | bytes 3145736 | tf_op jit(solution)/shard_map/ppermute | solution.py:137
  54.7 24.9 %copy-start.13 = (bf16[256,256]{1,0:T(8,128)(2,1)S(1)}, bf16[256,256]{1,0:T(8,128)(2,1)}, u32[]{:S(2)}) copy-start(bf16[256,256]{1,0:T(8,128)(2,1)} %param.13) | copy-start | bytes 393220
  100.4 7.5 %copy-start.1 = (bf16[8,288,256]{2,1,0:T(8,128)(2,1)}, bf16[8,288,256]{2,1,0:T(8,128)(2,1)S(1)}, u32[]{:S(2)}) copy-start(bf16[8,288,256]{2,1,0:T(8,128)(2,1)S(1)} %all_to_all.26.refs_0_) | copy-start | bytes 3538948
  100.4 2.8 %collective-permute-start.5 = (bf16[8,288,256]{2,1,0:T(8,128)(2,1)S(1)}, bf16[8,288,256]{2,1,0:T(8,128)(2,1)S(1)}, u32[]{:S(2)}, u32[]{:S(2)}) collective-permute-start(bf16[8,288,256]{2,1,0:T(8,128)(2,1)S(1)} %all_to_all.26.refs_0_), channel_id=1, source_target_pairs={{0,1},{1,0},{2,3},{3,2},{4,5},{5,4},{6,7},{7,6},{8,9},{9,8},{10,11... | collective-permute-start | bytes 3538952 | tf_op jit(solution)/shard_map/ppermute | solution.py:137
  103.2 4.7 %copy-start.8 = (bf16[8,288,256]{2,1,0:T(8,128)(2,1)}, bf16[8,288,256]{2,1,0:T(8,128)(2,1)S(1)}, u32[]{:S(2)}) copy-start(bf16[8,288,256]{2,1,0:T(8,128)(2,1)S(1)} %collective-permute-done.5.refs_1_) | copy-start | bytes 3538948
  104.1 17.4 %all-to-all-start.2 = ((f32[16,16,256]{2,1,0:T(8,128)}), f32[16,16,256]{2,1,0:T(8,128)S(1)}, u32[]{:S(2)}, u32[]{:S(2)}) async-start(f32[16,16,256]{2,1,0:T(8,128)} %broadcast_in_dim.35), calls=%async_computation.2 | async-start | bytes 524288 | tf_op jit(solution)/shard_map/all_to_all | solution.py:119
  113.7 22.0 %copy-start.5 = (bf16[512,256]{1,0:T(8,128)(2,1)S(1)}, bf16[512,256]{1,0:T(8,128)(2,1)}, u32[]{:S(2)}) copy-start(bf16[512,256]{1,0:T(8,128)(2,1)} %get-tuple-element.33) | copy-start | bytes 786436
  113.7 25.1 %copy-start.4 = (bf16[512,256]{1,0:T(8,128)(2,1)S(1)}, bf16[512,256]{1,0:T(8,128)(2,1)}, u32[]{:S(2)}) copy-start(bf16[512,256]{1,0:T(8,128)(2,1)} %get-tuple-element.24) | copy-start | bytes 786436
  121.6 14.1 %collective-permute-start.6 = (bf16[1024,256]{1,0:T(8,128)(2,1)}, bf16[1024,256]{1,0:T(8,128)(2,1)S(1)}, u32[]{:S(2)}, u32[]{:S(2)}) collective-permute-start(bf16[1024,256]{1,0:T(8,128)(2,1)} %get-tuple-element.28), channel_id=1, source_target_pairs={{0,64},{64,128},{128,192},{192,0},{1,65},{65,129},{129,193},{193,1... | collective-permute-start | bytes 1572872 | tf_op jit(solution)/shard_map/ppermute | solution.py:137
  121.6 14.1 %collective-permute-start.7 = (bf16[1024,256]{1,0:T(8,128)(2,1)}, bf16[1024,256]{1,0:T(8,128)(2,1)S(1)}, u32[]{:S(2)}, u32[]{:S(2)}) collective-permute-start(bf16[1024,256]{1,0:T(8,128)(2,1)} %get-tuple-element.29), channel_id=1, source_target_pairs={{0,192},{64,0},{128,64},{192,128},{1,193},{65,1},{129,65},{193,129... | collective-permute-start | bytes 1572872 | tf_op jit(solution)/shard_map/ppermute | solution.py:137
  124.8 21.7 %copy-start.3 = (bf16[1024,256]{1,0:T(8,128)(2,1)S(1)}, bf16[1024,256]{1,0:T(8,128)(2,1)}, u32[]{:S(2)}) copy-start(bf16[1024,256]{1,0:T(8,128)(2,1)} %get-tuple-element.23) | copy-start | bytes 1572868
  135.8 8.1 %collective-permute-start.9 = (bf16[512,256]{1,0:T(8,128)(2,1)S(1)}, bf16[512,256]{1,0:T(8,128)(2,1)S(1)}, u32[]{:S(2)}, u32[]{:S(2)}) collective-permute-start(bf16[512,256]{1,0:T(8,128)(2,1)S(1)} %add_convert_fusion.2), channel_id=1, source_target_pairs={{0,192},{64,0},{128,64},{192,128},{1,193},{65,1},{129,65},{193,129... | collective-permute-start | bytes 786440 | tf_op jit(solution)/shard_map/ppermute | solution.py:137
  138.9 7.7 %collective-permute-start.8 = (bf16[512,256]{1,0:T(8,128)(2,1)S(1)}, bf16[512,256]{1,0:T(8,128)(2,1)S(1)}, u32[]{:S(2)}, u32[]{:S(2)}) collective-permute-start(bf16[512,256]{1,0:T(8,128)(2,1)S(1)} %add_convert_fusion.4), channel_id=1, source_target_pairs={{0,64},{64,128},{128,192},{192,0},{1,65},{65,129},{129,193},{193,1... | collective-permute-start | bytes 786440 | tf_op jit(solution)/shard_map/ppermute | solution.py:137
  147.6 18.6 %all-to-all-start.4 = ((bf16[4,256,256]{2,1,0:T(8,128)(2,1)}), bf16[4,256,256]{2,1,0:T(8,128)(2,1)S(1)}, u32[]{:S(2)}, u32[]{:S(2)}) async-start(bf16[4,256,256]{2,1,0:T(8,128)(2,1)} %bitcast.10), calls=%async_computation.4 | async-start | bytes 1048576 | tf_op jit(solution)/shard_map/all_to_all | solution.py:119

commit v4 on v3

--- a/solution.py
+++ b/solution.py
@@ -12,17 +12,22 @@
     return jax.nn.gelu(value, approximate=True)
 
 
-def tile_kernel(count_ref, put_ref, take_ref, tiles_hbm, *refs, pieces, outs, group, transpose):
-    piece_refs, out_refs = refs[: len(pieces)], refs[len(pieces) : len(pieces) + len(outs)]
-    tiles_ref, source_ref, sum_ref, *rounded, tiles_in, source_in, out_sent = refs[len(pieces) + len(outs) :]
+def tile_kernel(count_ref, put_ref, slot_ref, take_ref, tiles_hbm, *refs, pieces, outs, group, transpose):
+    piece_refs, out_refs = refs[: len(pieces)], refs[len(pieces) : len(pieces) + outs]
+    tiles_ref, source_ref, sum_ref, *rounded, tiles_in, source_in, out_sent = refs[len(pieces) + outs :]
     size = tiles_ref.shape[-1]
-    spare = sum_ref.shape[0] // size - 1
-    live = count_ref[0]
+    batches = (count_ref[0] + group - 1) // group
+
+    def fetch(index):
+        for lane in range(2 * group):
+            place = index * 2 * group + lane
+            pltpu.make_async_copy(tiles_hbm.at[slot_ref[place]], tiles_ref.at[place], tiles_in.at[index]).start()
+
+    def fetched(index):
+        some = pl.ds(pl.multiple_of(index * 2 * group, 2 * group), 2 * group)
+        pltpu.make_async_copy(tiles_hbm.at[pl.ds(0, 2 * group)], tiles_ref.at[some], tiles_in.at[index]).wait()
+
     contract = (((0,), (0,)), ((), ())) if transpose else (((1,), (0,)), ((), ()))
-
-    def tiles_copy(index):
-        some = pl.ds(pl.multiple_of(index * group, group), group)
-        return pltpu.make_async_copy(tiles_hbm.at[some], tiles_ref.at[some], tiles_in.at[index])
 
     copies, at = [], 0
     for piece, (blocks, rows) in zip(piece_refs, pieces):
@@ -37,29 +42,33 @@
             at += rows
     for copy in copies:
         copy.start()
-    batches = (live + group - 1) // group
-
-    def begin(index, carry):
-        tiles_copy(index).start()
-        return carry
-
-    lax.fori_loop(0, batches, begin, 0)
+    fetch(0)
+    for index in range(1, AHEAD):
+        pl.when(index < batches)(functools.partial(fetch, index))
+    source_ref[pl.ds(at, size), :] = jnp.zeros((size, source_ref.shape[1]), source_ref.dtype)
     sum_ref[...] = jnp.zeros_like(sum_ref)
     for copy in copies:
         copy.wait()
 
     def batch(index, carry):
-        tiles_copy(index).wait()
+        pl.when(index + AHEAD < batches)(lambda: fetch(index + AHEAD))
+        fetched(index)
         rows, products = [], []
         for lane in range(group):
-            slot = index * group + lane
-            used = slot < live
-            put = jnp.where(used, put_ref[slot], spare)
-            take = jnp.where(used, take_ref[slot], 0)
-            picked = source_ref[pl.ds(pl.multiple_of(take * size, size), size), :]
-            rows.append(pl.multiple_of(put * size, size))
+            pair = index * group + lane
+            tiles, picked = [], []
+            for place in (2 * pair, 2 * pair + 1):
+                take = pl.multiple_of(take_ref[place] * size, size)
+                tiles.append(tiles_ref[place])
+                picked.append(source_ref[pl.ds(take, size), :])
+            rows.append(pl.multiple_of(put_ref[pair] * size, size))
             products.append(
-                lax.dot_general(tiles_ref[slot], picked, contract, preferred_element_type=jnp.float32)
+                lax.dot_general(
+                    jnp.concatenate(tiles, axis=0 if transpose else 1),
+                    jnp.concatenate(picked, axis=0),
+                    contract,
+                    preferred_element_type=jnp.float32,
+                )
             )
         for row, product in zip(rows, products):
             sum_ref[pl.ds(row, size), :] += product
@@ -68,51 +77,72 @@
     lax.fori_loop(0, batches, batch, 0)
 
     writes, at = [], 0
-    for out in out_refs:
-        part = sum_ref.at[pl.ds(at, out.shape[0]), :]
+    for out, narrow in zip(out_refs, rounded):
+        narrow[...] = sum_ref[pl.ds(at, out.shape[0]), :].astype(out.dtype)
+        writes.append(pltpu.make_async_copy(narrow, out, out_sent.at[len(writes)]))
+        writes[-1].start()
         at += out.shape[0]
-        if out.dtype != sum_ref.dtype:
-            narrow = rounded.pop(0)
-            narrow[...] = part[...].astype(out.dtype)
-            part = narrow
-        writes.append(pltpu.make_async_copy(part, out, out_sent.at[len(writes)]))
-        writes[-1].start()
     for write in writes:
         write.wait()
 
 
-def tile_products(live_count, put_ids, take_ids, block_tiles, sources, rows_used, outs, transpose):
+PAIRS_AT_ONCE = 16
+AHEAD = 4
+
+
+def pair_up(live_count, put_ids, take_ids, put_blocks, take_blocks):
+    slots = put_ids.shape[0]
+    slot = jnp.arange(slots, dtype=jnp.int32)
+    block = jnp.arange(put_blocks, dtype=jnp.int32)
+    put_ids = jnp.where(slot < live_count, put_ids, put_blocks)
+    rank = ((put_ids[:, None] == put_ids[None, :]) & (slot[None, :] < slot[:, None])).astype(jnp.int32).sum(1)
+    pairs_of = ((put_ids[:, None] == block[None, :]).astype(jnp.int32).sum(0) + 1) // 2
+    first = 2 * jnp.where(block[None, :] < put_ids[:, None], pairs_of[None, :], 0).sum(1)
+    place = jnp.where(put_ids < put_blocks, first + rank, -1)
+    pair_count = pairs_of.sum()
+    room = -(-(slots + put_blocks) // (2 * PAIRS_AT_ONCE)) * PAIRS_AT_ONCE
+    pair = jnp.arange(room, dtype=jnp.int32)
+    spot = jnp.arange(2 * room, dtype=jnp.int32)
+    here = place[None, :] == spot[:, None]
+    slot_ids = jnp.where(here, slot[None, :], 0).sum(1)
+    take_ids = jnp.where(here, take_ids[None, :] - take_blocks, 0).sum(1) + take_blocks
+    pair_put = jnp.where(place[None, :] == 2 * pair[:, None], put_ids[None, :] - put_blocks, 0).sum(1) + put_blocks
+    return pair_count.reshape(1), pair_put, slot_ids, take_ids
+
+
+def tile_products(pairs, block_tiles, sources, rows_used, outs, transpose):
     slots, size, _ = block_tiles.shape
     width = sources[0].shape[-1]
     sources = [source.reshape((-1,) + source.shape[-2:]) for source in sources]
     pieces = [(source.shape[0], rows_used or source.shape[1]) for source in sources]
     source_rows = sum(blocks * rows for blocks, rows in pieces)
-    sum_rows = sum(rows for rows, _ in outs)
-    group = math.gcd(slots, 32)
+    sum_rows = sum(outs)
+    places = pairs[2].shape[0]
     anywhere = pl.BlockSpec(memory_space=pl.ANY)
     return pl.pallas_call(
-        functools.partial(tile_kernel, pieces=pieces, outs=outs, group=group, transpose=transpose),
-        out_shape=[jax.ShapeDtypeStruct((rows, width), kind) for rows, kind in outs],
-        in_specs=[pl.BlockSpec(memory_space=pltpu.SMEM)] * 3 + [anywhere] * (1 + len(sources)),
+        functools.partial(tile_kernel, pieces=pieces, outs=len(outs), group=PAIRS_AT_ONCE, transpose=transpose),
+        out_shape=[jax.ShapeDtypeStruct((rows, width), jnp.bfloat16) for rows in outs],
+        in_specs=[pl.BlockSpec(memory_space=pltpu.SMEM)] * 4
+        + [anywhere] * (1 + len(sources)),
         out_specs=[anywhere] * len(outs),
         scratch_shapes=[
-            pltpu.VMEM((slots, size, size), jnp.bfloat16),
-            pltpu.VMEM((source_rows, width), jnp.bfloat16),
+            pltpu.VMEM((places, size, size), jnp.bfloat16),
+            pltpu.VMEM((source_rows + size, width), jnp.bfloat16),
             pltpu.VMEM((sum_rows + size, width), jnp.float32),
         ]
-        + [pltpu.VMEM((rows, width), kind) for rows, kind in outs if kind != jnp.float32]
+        + [pltpu.VMEM((rows, width), jnp.bfloat16) for rows in outs]
         + [
-            pltpu.SemaphoreType.DMA((slots // group,)),
+            pltpu.SemaphoreType.DMA((places // (2 * PAIRS_AT_ONCE),)),
             pltpu.SemaphoreType.DMA((sum(blocks for blocks, _ in pieces),)),
             pltpu.SemaphoreType.DMA((len(outs),)),
         ],
-        compiler_params=pltpu.CompilerParams(vmem_limit_bytes=56 << 20),
+        compiler_params=pltpu.CompilerParams(vmem_limit_bytes=(56 if transpose else 48) << 20),
         cost_estimate=pl.CostEstimate(
             flops=8 * slots * size * size * width,
             bytes_accessed=2 * slots * size * size + 4 * sum_rows * width,
             transcendentals=0,
         ),
-    )(live_count, put_ids, take_ids, block_tiles, *sources)
+    )(*pairs, block_tiles, *sources)
 
 
 def exchange(chunks, axes):
@@ -141,7 +171,7 @@
     seg_rows, feat_width = features.shape
     block_tiles = tile_values[0, 0]
     size = block_tiles.shape[-1]
-    live_count = tile_count[0]
+    live_count = tile_count[0, 0]
     tile_row_ids = tile_rows[0, 0]
     tile_col_ids = tile_cols[0, 0]
     far, near = lax.axis_size("row_far"), lax.axis_size("row_near")
@@ -180,12 +210,15 @@
         + tile_row_ids % seg_tiles
     )
 
+    row_tiles, col_tiles = lax.axis_size(col) * seg_tiles, lax.axis_size(row) * seg_tiles
+    row_pairs = pair_up(live_count, row_place, col_take, row_tiles, col_tiles)
+    col_pairs = pair_up(live_count, col_put, row_place, col_tiles, row_tiles)
+
     own = lax.all_gather(features, "row_near", axis=0, tiled=True)
     left, right = shift(own, "row_far", 1), shift(own, "row_far", -1)
     low, high = shift(left[:half_rows], "row_far", 1), shift(right[half_rows:], "row_far", -1)
     keep, send = tile_products(
-        live_count, row_place, col_take, block_tiles, [own, left, right, low, high], None,
-        [(mid_rows, jnp.bfloat16)] * 2, False,
+        row_pairs, block_tiles, [own, left, right, low, high], None, [mid_rows] * 2, False
     )
     paired = add(keep, shift(send, "col_near", 1))
     parts = exchange(paired.reshape(mid, seg_rows, feat_width), ("col_far", "col_mid"))
@@ -216,9 +249,7 @@
     weight_slices = exchange(weight_slices, row)
 
     own, right_one, left_one, right_two, left_two = tile_products(
-        live_count, col_put, row_place, block_tiles, [mine, theirs], seg_rows,
-        [(far_rows, jnp.bfloat16)] * 3 + [(half_rows, jnp.bfloat16)] * 2,
-        True,
+        col_pairs, block_tiles, [mine, theirs], seg_rows, [far_rows] * 3 + [half_rows] * 2, True
     )
     right_one, left_one, weight_slices = lax.optimization_barrier((right_one, left_one, weight_slices))
     from_left, from_right = shift(right_one, "row_far", 1), shift(left_one, "row_far", -1)

time: 170 us -> 166 us (0.976)
  the two profiles are of different devices: /device:TPU:2 before, /device:TPU:0 now
where the time goes in v4:
time: 166 us; the launch traced here: 164 us
  blocking collectives  73.4 us (44%)
  waiting for transfers between devices  45.3 us (27%)
  starting transfers between devices  22.5 us (14%)
  Pallas kernels  10.6 us (6%)
  other arithmetic  7.3 us (4%)
  matrix products  2.12 us (1%)
  local copies, waits for them, and re-layouts  1.68 us (1%)
    all_to_all x3, blocking collectives, exchange(): return lax.all_to_all(chunks, axes, 0, 0)  54.7 us
    ppermute x10, waiting for transfers between devices, shift(): lax.ppermute(block, axis, [(k, (k + by) % devices) for k in range(devices)])  23.2 us
    all_to_all x2, waiting for transfers between devices, exchange(): return lax.all_to_all(chunks, axes, 0, 0)  22.1 us
    all_gather x1, blocking collectives, on_device(): own = lax.all_gather(features, 'row_near', axis=0, tiled=True)  18.7 us
    ppermute x10, starting transfers between devices, shift(): lax.ppermute(block, axis, [(k, (k + by) % devices) for k in range(devices)])  13.2 us
    pallas_call x2, Pallas kernels, tile_products(): pl.pallas_call(functools.partial(tile_kernel, pieces=pieces, outs=len(out...  10.6 us
    all_to_all x2, starting transfers between devices, exchange(): return lax.all_to_all(chunks, axes, 0, 0)  9.33 us
  transfers between devices with their start and end apart: 12, of which 10 were waited for; matrix products, arithmetic and copies ran while one was open for 3% of the time, Pallas kernels for 4%

profile of v4, /device:TPU:0, one launch (start us, length us, event | category | flops | bytes accessed | tf_op | source)
XLA Modules:
  0.0 164.5 jit_solution(951773362054808794)
XLA Ops:
  0.6 0.0 copy-start
  0.6 18.7 %all_gather.3 = bf16[1024,256]{1,0:T(8,128)(2,1)S(1)} all-gather(bf16[256,256]{1,0:T(8,128)(2,1)} %param.7), channel_id=1, replica_groups=mesh['row_far'=4,'row_near'=4,'col_far'=4,'col_mid'=2,'col_near'=2] {'ro..., dimensions={0}, use_global_device_ids=true | all-gather | bytes 655360 | tf_op jit(solution)/shard_map/all_gather | solution.py:217
  19.3 3.0 %collective-permute-start.1 = (bf16[1024,256]{1,0:T(8,128)(2,1)S(1)}, bf16[1024,256]{1,0:T(8,128)(2,1)S(1)}, u32[]{:S(2)}, u32[]{:S(2)}) collective-permute-start(bf16[1024,256]{1,0:T(8,128)(2,1)S(1)} %all_gather.3), channel_id=1, source_target_pairs={{0,192},{64,0},{128,64},{192,128},{1,193},{65,1},{129,65},{193,129... | collective-permute-start | bytes 1572872 | tf_op jit(solution)/shard_map/ppermute | solution.py:167
  22.3 0.0 collective-permute-start
  23.0 0.7 reduce.3
  23.7 0.1 convert_reduce_fusion.4
  23.8 0.2 convert_reduce_fusion
  24.1 0.7 reduce.2
  24.8 0.1 convert_reduce_fusion.5
  24.9 0.2 convert_reduce_fusion.1
  25.1 0.7 fusion.24
  25.8 0.1 select_reduce_fusion.6
  25.9 0.1 select_reduce_fusion.7
  26.0 0.2 select_reduce_fusion.4
  26.3 4.5 %collective-permute-done.1 = bf16[1024,256]{1,0:T(8,128)(2,1)S(1)} collective-permute-done((bf16[1024,256]{1,0:T(8,128)(2,1)S(1)}, bf16[1024,256]{1,0:T(8,128)(2,1)S(1)}, u32[]{:S(2)}, u32[]{:S(2)}) %collective-permute-start.1) | collective-permute-done | bytes 524320 | tf_op jit(solution)/shard_map/ppermute | solution.py:167
  30.8 3.7 %collective-permute-start.3 = (bf16[512,256]{1,0:T(8,128)(2,1)S(1)}, bf16[512,256]{1,0:T(8,128)(2,1)S(1)}, u32[]{:S(2)}, u32[]{:S(2)}) collective-permute-start(bf16[512,256]{1,0:T(8,128)(2,1)S(1)} %slice.41), channel_id=1, source_target_pairs={{0,192},{64,0},{128,64},{192,128},{1,193},{65,1},{129,65},{193,129... | collective-permute-start | bytes 786440 | tf_op jit(solution)/shard_map/ppermute | solution.py:167
  34.5 0.0 collective-permute-done
  34.5 0.1 collective-permute-start.2
  34.6 0.2 select_reduce_fusion.2
  34.8 3.6 %collective-permute-done.3 = bf16[512,256]{1,0:T(8,128)(2,1)S(1)} collective-permute-done((bf16[512,256]{1,0:T(8,128)(2,1)S(1)}, bf16[512,256]{1,0:T(8,128)(2,1)S(1)}, u32[]{:S(2)}, u32[]{:S(2)}) %collective-permute-start.3) | collective-permute-done | bytes 262176 | tf_op jit(solution)/shard_map/ppermute | solution.py:167
  38.3 3.8 %collective-permute-done.2 = bf16[512,256]{1,0:T(8,128)(2,1)S(1)} collective-permute-done((bf16[512,256]{1,0:T(8,128)(2,1)S(1)}, bf16[512,256]{1,0:T(8,128)(2,1)S(1)}, u32[]{:S(2)}, u32[]{:S(2)}) %collective-permute-start.2) | collective-permute-done | bytes 262176 | tf_op jit(solution)/shard_map/ppermute | solution.py:167
  42.1 4.5 %shard_map.94 = (bf16[2048,256]{1,0:T(8,128)(2,1)S(1)}, bf16[2048,256]{1,0:T(8,128)(2,1)S(1)}) custom-call(s32[1]{0:T(128)} %bitcast.1.count_ref, s32[176]{0:T(256)S(1)} %broadcast_add_fusion.6.put_ref, s32[352]{0:T(512)S(1)} %get-tuple-element.38.slot_ref, s32[352]{0:T(512)S(1)} %broadcast_add_fusion.1.take_ref, bf16[320,128,128]{2,1,0:T(8,128)(2,1)} %bitcast.29, ...), custom_call_target="tpu_custom_call" | custom-call | flops 10737418240 | bytes 14680064 | tf_op jit(solution)/shard_map/pallas_call | solution.py:122
  46.6 0.1 collective-permute-start.4
  46.7 2.6 %collective-permute-done.4 = bf16[2048,256]{1,0:T(8,128)(2,1)S(1)} collective-permute-done((bf16[2048,256]{1,0:T(8,128)(2,1)S(1)}, bf16[2048,256]{1,0:T(8,128)(2,1)S(1)}, u32[]{:S(2)}, u32[]{:S(2)}) %collective-permute-start.4) | collective-permute-done | bytes 1048608 | tf_op jit(solution)/shard_map/ppermute | solution.py:167
  49.4 0.3 add_convert_fusion
  49.7 0.0 copy-start.6
  49.7 24.7 %all_to_all.25 = bf16[8,256,256]{2,1,0:T(8,128)(2,1)S(1)} all-to-all(bf16[8,256,256]{2,1,0:T(8,128)(2,1)S(1)} %bitcast.26), channel_id=1, replica_groups=mesh['row_far'=4,'row_near'=4,'col_far'=4,'col_mid'=2,'col_near'=2] {'co..., dimensions={0} | all-to-all | bytes 2097152 | tf_op jit(solution)/shard_map/all_to_all | solution.py:149
  74.3 0.1 reduce_sum.184
  74.5 0.0 copy-done
  74.5 0.0 copy-done.6
  74.5 1.0 fusion.4
  75.5 0.2 convolution_convert_fusion.1
  75.8 0.1 broadcast_in_dim.151
  75.8 0.1 pad_maximum_fusion
  75.9 19.3 %all_to_all.26.refs_0_ = bf16[8,288,256]{2,1,0:T(8,128)(2,1)S(1)} all-to-all(bf16[8,288,256]{2,1,0:T(8,128)(2,1)S(1)} %pad_maximum_fusion), channel_id=1, replica_groups=mesh['row_far'=4,'row_near'=4,'col_far'=4,'col_mid'=2,'col_near'=2] {'co..., dimensions={0} | all-to-all | bytes 2359296 | tf_op jit(solution)/shard_map/all_to_all | solution.py:149
  95.2 0.0 collective-permute-start.5
  95.2 0.9 select_reduce_fusion
  96.1 0.6 broadcast_add_fusion.5.put_ref
  96.7 0.6 broadcast_add_fusion.take_ref
  97.3 0.7 collective-permute-done.5.refs_1_
  98.1 0.8 broadcast_in_dim.152
  98.9 4.2 %all-to-all-start.2 = ((f32[16,16,256]{2,1,0:T(8,128)}), f32[16,16,256]{2,1,0:T(8,128)S(1)}, u32[]{:S(2)}, u32[]{:S(2)}) async-start(f32[16,16,256]{2,1,0:T(8,128)} %broadcast_in_dim.152), calls=%async_computation.2 | async-start | bytes 524288 | tf_op jit(solution)/shard_map/all_to_all | solution.py:149
  103.1 0.0 copy-done.1
  103.1 6.1 %shard_map.95 = (bf16[1024,256]{1,0:T(8,128)(2,1)}, bf16[1024,256]{1,0:T(8,128)(2,1)}, bf16[1024,256]{1,0:T(8,128)(2,1)}, bf16[512,256]{1,0:T(8,128)(2,1)}, bf16[512,256]{1,0:T(8,128)(2,1)}) custom-call(s32[1]{0:T(128)} %bitcast.9.count_ref, s32[176]{0:T(256)} %broadcast_add_fusion.5.put_ref, s32[352]{0:T(512)} %get-tuple-element.36.slot_ref, ...), custom_call_target="tpu_custom_call" | custom-call | flops 10737418240 | bytes 14680064 | tf_op jit(solution)/shard_map/pallas_call | solution.py:122
  109.2 0.0 copy-start.3
  109.3 7.1 %all-to-all-done.2 = f32[16,16,256]{2,1,0:T(8,128)S(1)} async-done(((f32[16,16,256]{2,1,0:T(8,128)}), f32[16,16,256]{2,1,0:T(8,128)S(1)}, u32[]{:S(2)}, u32[]{:S(2)}) %all-to-all-start.2) | async-done | bytes 262176 | tf_op jit(solution)/shard_map/all_to_all | solution.py:149
  116.4 0.0 collective-permute-start.6
  116.4 3.2 %collective-permute-start.7 = (bf16[1024,256]{1,0:T(8,128)(2,1)}, bf16[1024,256]{1,0:T(8,128)(2,1)S(1)}, u32[]{:S(2)}, u32[]{:S(2)}) collective-permute-start(bf16[1024,256]{1,0:T(8,128)(2,1)} %get-tuple-element.29), channel_id=1, source_target_pairs={{0,192},{64,0},{128,64},{192,128},{1,193},{65,1},{129,65},{193,129... | collective-permute-start | bytes 1572872 | tf_op jit(solution)/shard_map/ppermute | solution.py:167
  119.7 10.8 %all_to_all.27 = f32[16,16,256]{2,1,0:T(8,128)S(1)} all-to-all(f32[16,16,256]{2,1,0:T(8,128)S(1)} %broadcast_in_dim.153), channel_id=1, replica_groups=mesh['row_far'=4,'row_near'=4,'col_far'=4,'col_mid'=2,'col_near'=2] {'co..., dimensions={0} | all-to-all | bytes 524288 | tf_op jit(solution)/shard_map/all_to_all | solution.py:149
  130.5 0.4 collective-permute-done.6
  130.8 0.0 collective-permute-done.7
  130.8 0.1 add_convert_fusion.2
  130.9 3.0 %collective-permute-start.9 = (bf16[512,256]{1,0:T(8,128)(2,1)S(1)}, bf16[512,256]{1,0:T(8,128)(2,1)S(1)}, u32[]{:S(2)}, u32[]{:S(2)}) collective-permute-start(bf16[512,256]{1,0:T(8,128)(2,1)S(1)} %add_convert_fusion.2), channel_id=1, source_target_pairs={{0,192},{64,0},{128,64},{192,128},{1,193},{65,1},{129,65},{193,129... | collective-permute-start | bytes 786440 | tf_op jit(solution)/shard_map/ppermute | solution.py:167
  133.9 0.1 add_convert_fusion.4
  134.0 0.1 collective-permute-start.8
  134.1 4.2 %collective-permute-done.9 = bf16[512,256]{1,0:T(8,128)(2,1)S(1)} collective-permute-done((bf16[512,256]{1,0:T(8,128)(2,1)S(1)}, bf16[512,256]{1,0:T(8,128)(2,1)S(1)}, u32[]{:S(2)}, u32[]{:S(2)}) %collective-permute-start.9) | collective-permute-done | bytes 262176 | tf_op jit(solution)/shard_map/ppermute | solution.py:167
  138.4 3.3 %collective-permute-done.8 = bf16[512,256]{1,0:T(8,128)(2,1)S(1)} collective-permute-done((bf16[512,256]{1,0:T(8,128)(2,1)S(1)}, bf16[512,256]{1,0:T(8,128)(2,1)S(1)}, u32[]{:S(2)}, u32[]{:S(2)}) %collective-permute-start.8) | collective-permute-done | bytes 262176 | tf_op jit(solution)/shard_map/ppermute | solution.py:167
  141.7 0.2 add_convert_fusion.3
  141.9 0.8 pad_maximum_fusion.1
  142.7 5.2 %all-to-all-start.4 = ((bf16[4,256,256]{2,1,0:T(8,128)(2,1)}), bf16[4,256,256]{2,1,0:T(8,128)(2,1)S(1)}, u32[]{:S(2)}, u32[]{:S(2)}) async-start(bf16[4,256,256]{2,1,0:T(8,128)(2,1)} %bitcast.12), calls=%async_computation.4 | async-start | bytes 1048576 | tf_op jit(solution)/shard_map/all_to_all | solution.py:149
  147.9 15.0 %all-to-all-done.4 = bf16[4,256,256]{2,1,0:T(8,128)(2,1)S(1)} async-done(((bf16[4,256,256]{2,1,0:T(8,128)(2,1)}), bf16[4,256,256]{2,1,0:T(8,128)(2,1)S(1)}, u32[]{:S(2)}, u32[]{:S(2)}) %all-to-all-start.4) | async-done | bytes 524320 | tf_op jit(solution)/shard_map/all_to_all | solution.py:149
  162.8 0.1 reduce_sum.195
  162.9 0.9 convolution_convert_fusion
  163.8 0.7 copy.12
  (24 shorter events, 0.2 us)
Async XLA Ops:
  0.6 73.9 %copy-start = (bf16[256,256]{1,0:T(8,128)(2,1)S(1)}, bf16[256,256]{1,0:T(8,128)(2,1)}, u32[]{:S(2)}) copy-start(bf16[256,256]{1,0:T(8,128)(2,1)} %param.8) | copy-start | bytes 393220
  19.3 11.5 %collective-permute-start.1 = (bf16[1024,256]{1,0:T(8,128)(2,1)S(1)}, bf16[1024,256]{1,0:T(8,128)(2,1)S(1)}, u32[]{:S(2)}, u32[]{:S(2)}) collective-permute-start(bf16[1024,256]{1,0:T(8,128)(2,1)S(1)} %all_gather.3), channel_id=1, source_target_pairs={{0,192},{64,0},{128,64},{192,128},{1,193},{65,1},{129,65},{193,129... | collective-permute-start | bytes 1572872 | tf_op jit(solution)/shard_map/ppermute | solution.py:167
  22.3 12.1 %collective-permute-start = (bf16[1024,256]{1,0:T(8,128)(2,1)S(1)}, bf16[1024,256]{1,0:T(8,128)(2,1)S(1)}, u32[]{:S(2)}, u32[]{:S(2)}) collective-permute-start(bf16[1024,256]{1,0:T(8,128)(2,1)S(1)} %all_gather.3), channel_id=1, source_target_pairs={{0,64},{64,128},{128,192},{192,0},{1,65},{65,129},{129,193},{193,1... | collective-permute-start | bytes 1572872 | tf_op jit(solution)/shard_map/ppermute | solution.py:167
  30.8 7.6 %collective-permute-start.3 = (bf16[512,256]{1,0:T(8,128)(2,1)S(1)}, bf16[512,256]{1,0:T(8,128)(2,1)S(1)}, u32[]{:S(2)}, u32[]{:S(2)}) collective-permute-start(bf16[512,256]{1,0:T(8,128)(2,1)S(1)} %slice.41), channel_id=1, source_target_pairs={{0,192},{64,0},{128,64},{192,128},{1,193},{65,1},{129,65},{193,129... | collective-permute-start | bytes 786440 | tf_op jit(solution)/shard_map/ppermute | solution.py:167
  34.5 7.7 %collective-permute-start.2 = (bf16[512,256]{1,0:T(8,128)(2,1)S(1)}, bf16[512,256]{1,0:T(8,128)(2,1)S(1)}, u32[]{:S(2)}, u32[]{:S(2)}) collective-permute-start(bf16[512,256]{1,0:T(8,128)(2,1)S(1)} %slice.40), channel_id=1, source_target_pairs={{0,64},{64,128},{128,192},{192,0},{1,65},{65,129},{129,193},{193,1... | collective-permute-start | bytes 786440 | tf_op jit(solution)/shard_map/ppermute | solution.py:167
  46.6 2.7 %collective-permute-start.4 = (bf16[2048,256]{1,0:T(8,128)(2,1)S(1)}, bf16[2048,256]{1,0:T(8,128)(2,1)S(1)}, u32[]{:S(2)}, u32[]{:S(2)}) collective-permute-start(bf16[2048,256]{1,0:T(8,128)(2,1)S(1)} %get-tuple-element.20), channel_id=1, source_target_pairs={{0,1},{1,0},{2,3},{3,2},{4,5},{5,4},{6,7},{7,6},{8,9},{9,8},{10,11... | collective-permute-start | bytes 3145736 | tf_op jit(solution)/shard_map/ppermute | solution.py:167
  49.7 24.8 %copy-start.6 = (bf16[256,256]{1,0:T(8,128)(2,1)S(1)}, bf16[256,256]{1,0:T(8,128)(2,1)}, u32[]{:S(2)}) copy-start(bf16[256,256]{1,0:T(8,128)(2,1)} %param.13) | copy-start | bytes 393220
  95.2 7.9 %copy-start.1 = (bf16[8,288,256]{2,1,0:T(8,128)(2,1)}, bf16[8,288,256]{2,1,0:T(8,128)(2,1)S(1)}, u32[]{:S(2)}) copy-start(bf16[8,288,256]{2,1,0:T(8,128)(2,1)S(1)} %all_to_all.26.refs_0_) | copy-start | bytes 3538948
  95.2 2.8 %collective-permute-start.5 = (bf16[8,288,256]{2,1,0:T(8,128)(2,1)S(1)}, bf16[8,288,256]{2,1,0:T(8,128)(2,1)S(1)}, u32[]{:S(2)}, u32[]{:S(2)}) collective-permute-start(bf16[8,288,256]{2,1,0:T(8,128)(2,1)S(1)} %all_to_all.26.refs_0_), channel_id=1, source_target_pairs={{0,1},{1,0},{2,3},{3,2},{4,5},{5,4},{6,7},{7,6},{8,9},{9,8},{10,11... | collective-permute-start | bytes 3538952 | tf_op jit(solution)/shard_map/ppermute | solution.py:167
  98.0 5.0 %copy-start.5 = (bf16[8,288,256]{2,1,0:T(8,128)(2,1)}, bf16[8,288,256]{2,1,0:T(8,128)(2,1)S(1)}, u32[]{:S(2)}) copy-start(bf16[8,288,256]{2,1,0:T(8,128)(2,1)S(1)} %collective-permute-done.5.refs_1_) | copy-start | bytes 3538948
  98.9 17.5 %all-to-all-start.2 = ((f32[16,16,256]{2,1,0:T(8,128)}), f32[16,16,256]{2,1,0:T(8,128)S(1)}, u32[]{:S(2)}, u32[]{:S(2)}) async-start(f32[16,16,256]{2,1,0:T(8,128)} %broadcast_in_dim.152), calls=%async_computation.2 | async-start | bytes 524288 | tf_op jit(solution)/shard_map/all_to_all | solution.py:149
  109.2 21.6 %copy-start.4 = (bf16[512,256]{1,0:T(8,128)(2,1)S(1)}, bf16[512,256]{1,0:T(8,128)(2,1)}, u32[]{:S(2)}) copy-start(bf16[512,256]{1,0:T(8,128)(2,1)} %get-tuple-element.33) | copy-start | bytes 786436
  109.2 24.7 %copy-start.3 = (bf16[512,256]{1,0:T(8,128)(2,1)S(1)}, bf16[512,256]{1,0:T(8,128)(2,1)}, u32[]{:S(2)}) copy-start(bf16[512,256]{1,0:T(8,128)(2,1)} %get-tuple-element.24) | copy-start | bytes 786436
  116.4 14.5 %collective-permute-start.6 = (bf16[1024,256]{1,0:T(8,128)(2,1)}, bf16[1024,256]{1,0:T(8,128)(2,1)S(1)}, u32[]{:S(2)}, u32[]{:S(2)}) collective-permute-start(bf16[1024,256]{1,0:T(8,128)(2,1)} %get-tuple-element.28), channel_id=1, source_target_pairs={{0,64},{64,128},{128,192},{192,0},{1,65},{65,129},{129,193},{193,1... | collective-permute-start | bytes 1572872 | tf_op jit(solution)/shard_map/ppermute | solution.py:167
  116.4 14.5 %collective-permute-start.7 = (bf16[1024,256]{1,0:T(8,128)(2,1)}, bf16[1024,256]{1,0:T(8,128)(2,1)S(1)}, u32[]{:S(2)}, u32[]{:S(2)}) collective-permute-start(bf16[1024,256]{1,0:T(8,128)(2,1)} %get-tuple-element.29), channel_id=1, source_target_pairs={{0,192},{64,0},{128,64},{192,128},{1,193},{65,1},{129,65},{193,129... | collective-permute-start | bytes 1572872 | tf_op jit(solution)/shard_map/ppermute | solution.py:167
  119.7 22.0 %copy-start.2 = (bf16[1024,256]{1,0:T(8,128)(2,1)S(1)}, bf16[1024,256]{1,0:T(8,128)(2,1)}, u32[]{:S(2)}) copy-start(bf16[1024,256]{1,0:T(8,128)(2,1)} %get-tuple-element.23) | copy-start | bytes 1572868
  130.9 7.4 %collective-permute-start.9 = (bf16[512,256]{1,0:T(8,128)(2,1)S(1)}, bf16[512,256]{1,0:T(8,128)(2,1)S(1)}, u32[]{:S(2)}, u32[]{:S(2)}) collective-permute-start(bf16[512,256]{1,0:T(8,128)(2,1)S(1)} %add_convert_fusion.2), channel_id=1, source_target_pairs={{0,192},{64,0},{128,64},{192,128},{1,193},{65,1},{129,65},{193,129... | collective-permute-start | bytes 786440 | tf_op jit(solution)/shard_map/ppermute | solution.py:167
  134.0 7.7 %collective-permute-start.8 = (bf16[512,256]{1,0:T(8,128)(2,1)S(1)}, bf16[512,256]{1,0:T(8,128)(2,1)S(1)}, u32[]{:S(2)}, u32[]{:S(2)}) collective-permute-start(bf16[512,256]{1,0:T(8,128)(2,1)S(1)} %add_convert_fusion.4), channel_id=1, source_target_pairs={{0,64},{64,128},{128,192},{192,0},{1,65},{65,129},{129,193},{193,1... | collective-permute-start | bytes 786440 | tf_op jit(solution)/shard_map/ppermute | solution.py:167
  142.7 20.1 %all-to-all-start.4 = ((bf16[4,256,256]{2,1,0:T(8,128)(2,1)}), bf16[4,256,256]{2,1,0:T(8,128)(2,1)S(1)}, u32[]{:S(2)}, u32[]{:S(2)}) async-start(bf16[4,256,256]{2,1,0:T(8,128)(2,1)} %bitcast.12), calls=%async_computation.4 | async-start | bytes 1048576 | tf_op jit(solution)/shard_map/all_to_all | solution.py:149

commit v5 on v4

--- a/solution.py
+++ b/solution.py
@@ -244,6 +244,7 @@
     weight_pair = total(mine[:, seg_rows:]) + total(theirs[:, seg_rows:])
     weight_rows = feat_width // lax.axis_size(col)
     weight_slice = lax.dynamic_slice_in_dim(weight_pair, lax.axis_index("col_near") * weight_rows, weight_rows, 0)
+    weight_slice = weight_slice.astype(jnp.bfloat16)
     weight_slices = jnp.broadcast_to(weight_slice[None], (lax.axis_size(row),) + weight_slice.shape)
     mine, theirs, weight_slices = lax.optimization_barrier((mine, theirs, weight_slices))
     weight_slices = exchange(weight_slices, row)
@@ -254,7 +255,7 @@
     right_one, left_one, weight_slices = lax.optimization_barrier((right_one, left_one, weight_slices))
     from_left, from_right = shift(right_one, "row_far", 1), shift(left_one, "row_far", -1)
     weight_slice = total(weight_slices) * (1.0 / math.sqrt(node_total))
-    weight_grad = spread(weight_slice, col).reshape(feat_width, feat_width)
+    weight_grad = spread(weight_slice.astype(jnp.bfloat16), col).reshape(feat_width, feat_width)
     from_left, from_right, weight_grad = lax.optimization_barrier((from_left, from_right, weight_grad))
     right_two, left_two = add(right_two, from_left[:half_rows]), add(left_two, from_right[half_rows:])
     low, high = shift(right_two, "row_far", 1), shift(left_two, "row_far", -1)
@@ -267,7 +268,7 @@
     feature_grad = lax.dot_general(
         back_sum, weight, (((1,), (1,)), ((), ())), preferred_element_type=jnp.float32
     ).astype(jnp.bfloat16)
-    return (activations, feature_grad, weight_grad)
+    return (activations, feature_grad, weight_grad.astype(jnp.float32))
 
 
 def solution(mesh):

time: 166 us -> 167 us (level)
  the two profiles are of different devices: /device:TPU:0 before, /device:TPU:2 now
where the time goes in v5:
time: 167 us; the launch traced here: 165 us
  blocking collectives  70.4 us (42%)
  waiting for transfers between devices  40.6 us (24%)
  starting transfers between devices  26.4 us (16%)
  Pallas kernels  14.3 us (9%)
  other arithmetic  8.94 us (5%)
  matrix products  2.12 us (1%)
    all_to_all x3, blocking collectives, exchange(): return lax.all_to_all(chunks, axes, 0, 0)  50 us
    ppermute x10, waiting for transfers between devices, shift(): lax.ppermute(block, axis, [(k, (k + by) % devices) for k in range(devices)])  24.9 us
    all_gather x1, blocking collectives, on_device(): own = lax.all_gather(features, 'row_near', axis=0, tiled=True)  20.4 us
    all_to_all x2, waiting for transfers between devices, exchange(): return lax.all_to_all(chunks, axes, 0, 0)  15.7 us
    pallas_call x2, Pallas kernels, tile_products(): pl.pallas_call(functools.partial(tile_kernel, pieces=pieces, outs=len(out...  14.3 us
    ppermute x10, starting transfers between devices, shift(): lax.ppermute(block, axis, [(k, (k + by) % devices) for k in range(devices)])  13.3 us
    all_to_all x2, starting transfers between devices, exchange(): return lax.all_to_all(chunks, axes, 0, 0)  13.1 us
  transfers between devices with their start and end apart: 12, of which 10 were waited for; matrix products, arithmetic and copies ran while one was open for 4% of the time, Pallas kernels for 5%

profile of v5, /device:TPU:2, one launch (start us, length us, event | category | flops | bytes accessed | tf_op | source)
XLA Modules:
  0.0 165.2 jit_solution(8230594370173562623)
XLA Ops:
  0.6 0.0 copy-start
  0.6 20.4 %all_gather.3 = bf16[1024,256]{1,0:T(8,128)(2,1)S(1)} all-gather(bf16[256,256]{1,0:T(8,128)(2,1)} %param.7), channel_id=1, replica_groups=mesh['row_far'=4,'row_near'=4,'col_far'=4,'col_mid'=2,'col_near'=2] {'ro..., dimensions={0}, use_global_device_ids=true | all-gather | bytes 655360 | tf_op jit(solution)/shard_map/all_gather | solution.py:217
  21.1 3.0 %collective-permute-start.1 = (bf16[1024,256]{1,0:T(8,128)(2,1)S(1)}, bf16[1024,256]{1,0:T(8,128)(2,1)S(1)}, u32[]{:S(2)}, u32[]{:S(2)}) collective-permute-start(bf16[1024,256]{1,0:T(8,128)(2,1)S(1)} %all_gather.3), channel_id=1, source_target_pairs={{0,192},{64,0},{128,64},{192,128},{1,193},{65,1},{129,65},{193,129... | collective-permute-start | bytes 1572872 | tf_op jit(solution)/shard_map/ppermute | solution.py:167
  24.1 0.0 collective-permute-start
  24.7 0.7 reduce.3
  25.5 0.1 convert_reduce_fusion.5
  25.6 0.2 convert_reduce_fusion
  25.8 0.7 reduce.2
  26.5 0.1 convert_reduce_fusion.6
  26.7 0.2 convert_reduce_fusion.1
  26.9 0.7 fusion.25
  27.5 0.1 select_reduce_fusion.6
  27.6 0.1 select_reduce_fusion.7
  27.7 0.2 select_reduce_fusion.4
  28.0 4.5 %collective-permute-done.1 = bf16[1024,256]{1,0:T(8,128)(2,1)S(1)} collective-permute-done((bf16[1024,256]{1,0:T(8,128)(2,1)S(1)}, bf16[1024,256]{1,0:T(8,128)(2,1)S(1)}, u32[]{:S(2)}, u32[]{:S(2)}) %collective-permute-start.1) | collective-permute-done | bytes 524320 | tf_op jit(solution)/shard_map/ppermute | solution.py:167
  32.5 3.7 %collective-permute-start.3 = (bf16[512,256]{1,0:T(8,128)(2,1)S(1)}, bf16[512,256]{1,0:T(8,128)(2,1)S(1)}, u32[]{:S(2)}, u32[]{:S(2)}) collective-permute-start(bf16[512,256]{1,0:T(8,128)(2,1)S(1)} %slice.41), channel_id=1, source_target_pairs={{0,192},{64,0},{128,64},{192,128},{1,193},{65,1},{129,65},{193,129... | collective-permute-start | bytes 786440 | tf_op jit(solution)/shard_map/ppermute | solution.py:167
  36.2 0.0 collective-permute-done
  36.2 0.1 collective-permute-start.2
  36.3 0.2 select_reduce_fusion.2
  36.5 3.6 %collective-permute-done.3 = bf16[512,256]{1,0:T(8,128)(2,1)S(1)} collective-permute-done((bf16[512,256]{1,0:T(8,128)(2,1)S(1)}, bf16[512,256]{1,0:T(8,128)(2,1)S(1)}, u32[]{:S(2)}, u32[]{:S(2)}) %collective-permute-start.3) | collective-permute-done | bytes 262176 | tf_op jit(solution)/shard_map/ppermute | solution.py:167
  40.1 3.8 %collective-permute-done.2 = bf16[512,256]{1,0:T(8,128)(2,1)S(1)} collective-permute-done((bf16[512,256]{1,0:T(8,128)(2,1)S(1)}, bf16[512,256]{1,0:T(8,128)(2,1)S(1)}, u32[]{:S(2)}, u32[]{:S(2)}) %collective-permute-start.2) | collective-permute-done | bytes 262176 | tf_op jit(solution)/shard_map/ppermute | solution.py:167
  43.9 6.3 %shard_map.94 = (bf16[2048,256]{1,0:T(8,128)(2,1)S(1)}, bf16[2048,256]{1,0:T(8,128)(2,1)S(1)}) custom-call(s32[1]{0:T(128)} %bitcast.1.count_ref, s32[176]{0:T(256)S(1)} %broadcast_add_fusion.6.put_ref, s32[352]{0:T(512)S(1)} %get-tuple-element.38.slot_ref, s32[352]{0:T(512)S(1)} %broadcast_add_fusion.1.take_ref, bf16[320,128,128]{2,1,0:T(8,128)(2,1)} %bitcast.29, ...), custom_call_target="tpu_custom_call" | custom-call | flops 10737418240 | bytes 14680064 | tf_op jit(solution)/shard_map/pallas_call | solution.py:122
  50.2 0.1 collective-permute-start.4
  50.3 2.6 %collective-permute-done.4 = bf16[2048,256]{1,0:T(8,128)(2,1)S(1)} collective-permute-done((bf16[2048,256]{1,0:T(8,128)(2,1)S(1)}, bf16[2048,256]{1,0:T(8,128)(2,1)S(1)}, u32[]{:S(2)}, u32[]{:S(2)}) %collective-permute-start.4) | collective-permute-done | bytes 1048608 | tf_op jit(solution)/shard_map/ppermute | solution.py:167
  53.0 0.3 add_convert_fusion
  53.2 0.0 copy-start.5
  53.3 21.2 %all_to_all.25 = bf16[8,256,256]{2,1,0:T(8,128)(2,1)S(1)} all-to-all(bf16[8,256,256]{2,1,0:T(8,128)(2,1)S(1)} %bitcast.26), channel_id=1, replica_groups=mesh['row_far'=4,'row_near'=4,'col_far'=4,'col_mid'=2,'col_near'=2] {'co..., dimensions={0} | all-to-all | bytes 2097152 | tf_op jit(solution)/shard_map/all_to_all | solution.py:149
  74.5 0.1 reduce_sum.184
  74.6 0.0 copy-done
  74.6 0.0 copy-done.5
  74.7 1.0 fusion.4
  75.7 0.2 convolution_convert_fusion.1
  75.9 0.1 broadcast_in_dim.151
  76.0 0.1 pad_maximum_fusion
  76.1 19.4 %all_to_all.26.refs_0_ = bf16[8,288,256]{2,1,0:T(8,128)(2,1)S(1)} all-to-all(bf16[8,288,256]{2,1,0:T(8,128)(2,1)S(1)} %pad_maximum_fusion), channel_id=1, replica_groups=mesh['row_far'=4,'row_near'=4,'col_far'=4,'col_mid'=2,'col_near'=2] {'co..., dimensions={0} | all-to-all | bytes 2359296 | tf_op jit(solution)/shard_map/all_to_all | solution.py:149
  95.5 0.0 collective-permute-start.5
  95.5 0.9 select_reduce_fusion
  96.4 0.6 broadcast_add_fusion.5.put_ref
  97.0 0.6 broadcast_add_fusion.take_ref
  97.6 0.7 collective-permute-done.5.refs_1_
  98.4 0.8 broadcast_in_dim.152
  99.1 5.5 %all-to-all-start.2 = ((bf16[16,16,256]{2,1,0:T(8,128)(2,1)}), bf16[16,16,256]{2,1,0:T(8,128)(2,1)S(1)}, u32[]{:S(2)}, u32[]{:S(2)}) async-start(bf16[16,16,256]{2,1,0:T(8,128)(2,1)} %broadcast_in_dim.152), calls=%async_computation.2 | async-start | bytes 262144 | tf_op jit(solution)/shard_map/all_to_all | solution.py:149
  104.7 7.9 %shard_map.95 = (bf16[1024,256]{1,0:T(8,128)(2,1)}, bf16[1024,256]{1,0:T(8,128)(2,1)}, bf16[1024,256]{1,0:T(8,128)(2,1)}, bf16[512,256]{1,0:T(8,128)(2,1)}, bf16[512,256]{1,0:T(8,128)(2,1)}) custom-call(s32[1]{0:T(128)} %bitcast.9.count_ref, s32[176]{0:T(256)} %broadcast_add_fusion.5.put_ref, s32[352]{0:T(512)} %get-tuple-element.36.slot_ref, ...), custom_call_target="tpu_custom_call" | custom-call | flops 10737418240 | bytes 14680064 | tf_op jit(solution)/shard_map/pallas_call | solution.py:122
  112.6 0.0 copy-start.3
  112.6 3.0 %all-to-all-done.2 = bf16[16,16,256]{2,1,0:T(8,128)(2,1)S(1)} async-done(((bf16[16,16,256]{2,1,0:T(8,128)(2,1)}), bf16[16,16,256]{2,1,0:T(8,128)(2,1)S(1)}, u32[]{:S(2)}, u32[]{:S(2)}) %all-to-all-start.2) | async-done | bytes 131104 | tf_op jit(solution)/shard_map/all_to_all | solution.py:149
  115.6 1.6 collective-permute-start.6
  117.2 1.6 collective-permute-start.7
  118.9 9.4 %all_to_all.27 = bf16[16,16,256]{2,1,0:T(8,128)(2,1)S(1)} all-to-all(bf16[16,16,256]{2,1,0:T(8,128)(2,1)S(1)} %broadcast_in_dim.153), channel_id=1, replica_groups=mesh['row_far'=4,'row_near'=4,'col_far'=4,'col_mid'=2,'col_near'=2] {'co..., dimensions={0} | all-to-all | bytes 262144 | tf_op jit(solution)/shard_map/all_to_all | solution.py:149
  128.3 2.0 %collective-permute-done.6 = bf16[1024,256]{1,0:T(8,128)(2,1)S(1)} collective-permute-done((bf16[1024,256]{1,0:T(8,128)(2,1)}, bf16[1024,256]{1,0:T(8,128)(2,1)S(1)}, u32[]{:S(2)}, u32[]{:S(2)}) %collective-permute-start.6) | collective-permute-done | bytes 524320 | tf_op jit(solution)/shard_map/ppermute | solution.py:167
  130.3 0.0 collective-permute-done.7
  130.3 1.0 add_convert_fusion.2
  131.3 3.1 %collective-permute-start.9 = (bf16[512,256]{1,0:T(8,128)(2,1)S(1)}, bf16[512,256]{1,0:T(8,128)(2,1)S(1)}, u32[]{:S(2)}, u32[]{:S(2)}) collective-permute-start(bf16[512,256]{1,0:T(8,128)(2,1)S(1)} %add_convert_fusion.2), channel_id=1, source_target_pairs={{0,192},{64,0},{128,64},{192,128},{1,193},{65,1},{129,65},{193,129... | collective-permute-start | bytes 786440 | tf_op jit(solution)/shard_map/ppermute | solution.py:167
  134.4 0.0 copy-done.3
  134.4 0.1 add_convert_fusion.4
  134.5 0.1 collective-permute-start.8
  134.6 3.9 %collective-permute-done.9 = bf16[512,256]{1,0:T(8,128)(2,1)S(1)} collective-permute-done((bf16[512,256]{1,0:T(8,128)(2,1)S(1)}, bf16[512,256]{1,0:T(8,128)(2,1)S(1)}, u32[]{:S(2)}, u32[]{:S(2)}) %collective-permute-start.9) | collective-permute-done | bytes 262176 | tf_op jit(solution)/shard_map/ppermute | solution.py:167
  138.5 3.7 %collective-permute-done.8 = bf16[512,256]{1,0:T(8,128)(2,1)S(1)} collective-permute-done((bf16[512,256]{1,0:T(8,128)(2,1)S(1)}, bf16[512,256]{1,0:T(8,128)(2,1)S(1)}, u32[]{:S(2)}, u32[]{:S(2)}) %collective-permute-start.8) | collective-permute-done | bytes 262176 | tf_op jit(solution)/shard_map/ppermute | solution.py:167
  142.1 0.2 add_convert_fusion.3
  142.3 0.8 pad_maximum_fusion.1
  143.2 7.6 %all-to-all-start.4 = ((bf16[4,256,256]{2,1,0:T(8,128)(2,1)}), bf16[4,256,256]{2,1,0:T(8,128)(2,1)S(1)}, u32[]{:S(2)}, u32[]{:S(2)}) async-start(bf16[4,256,256]{2,1,0:T(8,128)(2,1)} %bitcast.12), calls=%async_computation.4 | async-start | bytes 1048576 | tf_op jit(solution)/shard_map/all_to_all | solution.py:149
  150.8 0.7 convert_element_type.136
  151.5 12.7 %all-to-all-done.4 = bf16[4,256,256]{2,1,0:T(8,128)(2,1)S(1)} async-done(((bf16[4,256,256]{2,1,0:T(8,128)(2,1)}), bf16[4,256,256]{2,1,0:T(8,128)(2,1)S(1)}, u32[]{:S(2)}, u32[]{:S(2)}) %all-to-all-start.4) | async-done | bytes 524320 | tf_op jit(solution)/shard_map/all_to_all | solution.py:149
  164.2 0.1 reduce_sum.195
  164.3 0.9 convolution_convert_fusion
  (22 shorter events, 0.2 us)
Async XLA Ops:
  0.6 74.0 %copy-start = (bf16[256,256]{1,0:T(8,128)(2,1)S(1)}, bf16[256,256]{1,0:T(8,128)(2,1)}, u32[]{:S(2)}) copy-start(bf16[256,256]{1,0:T(8,128)(2,1)} %param.8) | copy-start | bytes 393220
  21.1 11.5 %collective-permute-start.1 = (bf16[1024,256]{1,0:T(8,128)(2,1)S(1)}, bf16[1024,256]{1,0:T(8,128)(2,1)S(1)}, u32[]{:S(2)}, u32[]{:S(2)}) collective-permute-start(bf16[1024,256]{1,0:T(8,128)(2,1)S(1)} %all_gather.3), channel_id=1, source_target_pairs={{0,192},{64,0},{128,64},{192,128},{1,193},{65,1},{129,65},{193,129... | collective-permute-start | bytes 1572872 | tf_op jit(solution)/shard_map/ppermute | solution.py:167
  24.1 12.1 %collective-permute-start = (bf16[1024,256]{1,0:T(8,128)(2,1)S(1)}, bf16[1024,256]{1,0:T(8,128)(2,1)S(1)}, u32[]{:S(2)}, u32[]{:S(2)}) collective-permute-start(bf16[1024,256]{1,0:T(8,128)(2,1)S(1)} %all_gather.3), channel_id=1, source_target_pairs={{0,64},{64,128},{128,192},{192,0},{1,65},{65,129},{129,193},{193,1... | collective-permute-start | bytes 1572872 | tf_op jit(solution)/shard_map/ppermute | solution.py:167
  32.5 7.6 %collective-permute-start.3 = (bf16[512,256]{1,0:T(8,128)(2,1)S(1)}, bf16[512,256]{1,0:T(8,128)(2,1)S(1)}, u32[]{:S(2)}, u32[]{:S(2)}) collective-permute-start(bf16[512,256]{1,0:T(8,128)(2,1)S(1)} %slice.41), channel_id=1, source_target_pairs={{0,192},{64,0},{128,64},{192,128},{1,193},{65,1},{129,65},{193,129... | collective-permute-start | bytes 786440 | tf_op jit(solution)/shard_map/ppermute | solution.py:167
  36.2 7.7 %collective-permute-start.2 = (bf16[512,256]{1,0:T(8,128)(2,1)S(1)}, bf16[512,256]{1,0:T(8,128)(2,1)S(1)}, u32[]{:S(2)}, u32[]{:S(2)}) collective-permute-start(bf16[512,256]{1,0:T(8,128)(2,1)S(1)} %slice.40), channel_id=1, source_target_pairs={{0,64},{64,128},{128,192},{192,0},{1,65},{65,129},{129,193},{193,1... | collective-permute-start | bytes 786440 | tf_op jit(solution)/shard_map/ppermute | solution.py:167
  50.2 2.7 %collective-permute-start.4 = (bf16[2048,256]{1,0:T(8,128)(2,1)S(1)}, bf16[2048,256]{1,0:T(8,128)(2,1)S(1)}, u32[]{:S(2)}, u32[]{:S(2)}) collective-permute-start(bf16[2048,256]{1,0:T(8,128)(2,1)S(1)} %get-tuple-element.20), channel_id=1, source_target_pairs={{0,1},{1,0},{2,3},{3,2},{4,5},{5,4},{6,7},{7,6},{8,9},{9,8},{10,11... | collective-permute-start | bytes 3145736 | tf_op jit(solution)/shard_map/ppermute | solution.py:167
  53.2 21.4 %copy-start.5 = (bf16[256,256]{1,0:T(8,128)(2,1)S(1)}, bf16[256,256]{1,0:T(8,128)(2,1)}, u32[]{:S(2)}) copy-start(bf16[256,256]{1,0:T(8,128)(2,1)} %param.13) | copy-start | bytes 393220
  95.5 9.2 %copy-start.1 = (bf16[8,288,256]{2,1,0:T(8,128)(2,1)}, bf16[8,288,256]{2,1,0:T(8,128)(2,1)S(1)}, u32[]{:S(2)}) copy-start(bf16[8,288,256]{2,1,0:T(8,128)(2,1)S(1)} %all_to_all.26.refs_0_) | copy-start | bytes 3538948
  95.5 2.8 %collective-permute-start.5 = (bf16[8,288,256]{2,1,0:T(8,128)(2,1)S(1)}, bf16[8,288,256]{2,1,0:T(8,128)(2,1)S(1)}, u32[]{:S(2)}, u32[]{:S(2)}) collective-permute-start(bf16[8,288,256]{2,1,0:T(8,128)(2,1)S(1)} %all_to_all.26.refs_0_), channel_id=1, source_target_pairs={{0,1},{1,0},{2,3},{3,2},{4,5},{5,4},{6,7},{7,6},{8,9},{9,8},{10,11... | collective-permute-start | bytes 3538952 | tf_op jit(solution)/shard_map/ppermute | solution.py:167
  98.3 6.3 %copy-start.4 = (bf16[8,288,256]{2,1,0:T(8,128)(2,1)}, bf16[8,288,256]{2,1,0:T(8,128)(2,1)S(1)}, u32[]{:S(2)}) copy-start(bf16[8,288,256]{2,1,0:T(8,128)(2,1)S(1)} %collective-permute-done.5.refs_1_) | copy-start | bytes 3538948
  99.1 16.5 %all-to-all-start.2 = ((bf16[16,16,256]{2,1,0:T(8,128)(2,1)}), bf16[16,16,256]{2,1,0:T(8,128)(2,1)S(1)}, u32[]{:S(2)}, u32[]{:S(2)}) async-start(bf16[16,16,256]{2,1,0:T(8,128)(2,1)} %broadcast_in_dim.152), calls=%async_computation.2 | async-start | bytes 262144 | tf_op jit(solution)/shard_map/all_to_all | solution.py:149
  112.6 21.8 %copy-start.3 = (bf16[512,256]{1,0:T(8,128)(2,1)S(1)}, bf16[512,256]{1,0:T(8,128)(2,1)}, u32[]{:S(2)}) copy-start(bf16[512,256]{1,0:T(8,128)(2,1)} %get-tuple-element.24) | copy-start | bytes 786436
  112.6 29.6 %copy-start.2 = (bf16[1024,256]{1,0:T(8,128)(2,1)S(1)}, bf16[1024,256]{1,0:T(8,128)(2,1)}, u32[]{:S(2)}) copy-start(bf16[1024,256]{1,0:T(8,128)(2,1)} %get-tuple-element.23) | copy-start | bytes 1572868
  115.6 14.7 %collective-permute-start.6 = (bf16[1024,256]{1,0:T(8,128)(2,1)}, bf16[1024,256]{1,0:T(8,128)(2,1)S(1)}, u32[]{:S(2)}, u32[]{:S(2)}) collective-permute-start(bf16[1024,256]{1,0:T(8,128)(2,1)} %get-tuple-element.28), channel_id=1, source_target_pairs={{0,64},{64,128},{128,192},{192,0},{1,65},{65,129},{129,193},{193,1... | collective-permute-start | bytes 1572872 | tf_op jit(solution)/shard_map/ppermute | solution.py:167
  117.2 13.1 %collective-permute-start.7 = (bf16[1024,256]{1,0:T(8,128)(2,1)}, bf16[1024,256]{1,0:T(8,128)(2,1)S(1)}, u32[]{:S(2)}, u32[]{:S(2)}) collective-permute-start(bf16[1024,256]{1,0:T(8,128)(2,1)} %get-tuple-element.29), channel_id=1, source_target_pairs={{0,192},{64,0},{128,64},{192,128},{1,193},{65,1},{129,65},{193,129... | collective-permute-start | bytes 1572872 | tf_op jit(solution)/shard_map/ppermute | solution.py:167
  131.3 7.2 %collective-permute-start.9 = (bf16[512,256]{1,0:T(8,128)(2,1)S(1)}, bf16[512,256]{1,0:T(8,128)(2,1)S(1)}, u32[]{:S(2)}, u32[]{:S(2)}) collective-permute-start(bf16[512,256]{1,0:T(8,128)(2,1)S(1)} %add_convert_fusion.2), channel_id=1, source_target_pairs={{0,192},{64,0},{128,64},{192,128},{1,193},{65,1},{129,65},{193,129... | collective-permute-start | bytes 786440 | tf_op jit(solution)/shard_map/ppermute | solution.py:167
  134.5 7.7 %collective-permute-start.8 = (bf16[512,256]{1,0:T(8,128)(2,1)S(1)}, bf16[512,256]{1,0:T(8,128)(2,1)S(1)}, u32[]{:S(2)}, u32[]{:S(2)}) collective-permute-start(bf16[512,256]{1,0:T(8,128)(2,1)S(1)} %add_convert_fusion.4), channel_id=1, source_target_pairs={{0,64},{64,128},{128,192},{192,0},{1,65},{65,129},{129,193},{193,1... | collective-permute-start | bytes 786440 | tf_op jit(solution)/shard_map/ppermute | solution.py:167
  143.2 21.1 %all-to-all-start.4 = ((bf16[4,256,256]{2,1,0:T(8,128)(2,1)}), bf16[4,256,256]{2,1,0:T(8,128)(2,1)S(1)}, u32[]{:S(2)}, u32[]{:S(2)}) async-start(bf16[4,256,256]{2,1,0:T(8,128)(2,1)} %bitcast.12), calls=%async_computation.4 | async-start | bytes 1048576 | tf_op jit(solution)/shard_map/all_to_all | solution.py:149
